TPU v7x, 128 devices: a whole 4x4x4 slice. The times are simulated.
128 devices in a mesh: row: 8 (over y, z_hi), col: 16 (over x, z_lo, core).
Axes of the slice: x: 4, y: 4, z: 4 (z_hi: 2, z_lo: 2; z = z_hi * 2 + z_lo), core: 2. Of those that a mesh axis runs over, the one named last changes fastest.
Arguments:
- band_factors: bfloat16 [48, 48, 8, 256], P('col'), may hold values from -6 to 6
- pair_density: bfloat16 [48, 48, 16, 256], P('col'), may hold values from -6 to 6
- screened: bfloat16 [48, 48, 256, 256], P('col'), may hold values from -1 to 3, as said below
- coulomb: float32 [256], replicated, may hold values from 0.2 to 2
- window_mask: int32 [3, 48, 48], P(None, 'row'), may hold values 0 or 1
- trial_vector: bfloat16 [16, 48, 48], P(None, 'col'), may hold values from -0.0013809204 to 0.0013809204
Outputs:
- row_image: float32 [16, 3, 48], P('col', None, 'row')
- col_image: float32 [16, 48, 48], P(None, 'col', 'row')
Inputs may be any that keep to these rules, and one draw needn't show every extreme that they name: `screened`: every block is symmetric.
All inputs are finite; a program needn't handle non-finite values. No bound on the sum of `window_mask` on one device may be relied on, other than what follows from the above.
Results may differ from a plain program's by a relative error of at most 0.0041.
Values may be sent and summed in bfloat16 or wider, within the bound.
A program may use at most 192 MiB of HBM per device.

v0:
```python
import jax
import jax.numpy as jnp
from jax import lax
from jax.sharding import PartitionSpec as P

HIGHEST_PRECISION = lax.Precision.HIGHEST


def broadcast(block, axis, holder):
    block = jnp.where(lax.axis_index(axis) == holder, block, jnp.zeros_like(block))
    return lax.psum(block, axis)


def shifted(block, axis, distance):
    devices = range(lax.axis_size(axis))
    route = [(i - distance, i) for i in devices if i - distance in devices]
    return lax.ppermute(block, axis, route)


def slab_terms(
    row_bands,
    row_pairs,
    row_trial,
    row_lines,
    first_b,
    col_bands,
    col_pairs,
    col_trial,
    col_lines,
    blocks,
    q_values,
    kept_mask,
    coulomb,
):
    line_count, row_width = (row_bands.shape[0], row_bands.shape[1])
    mesh_side = col_bands.shape[1]
    band_half = row_bands.shape[2] // 2
    fourier = row_bands.shape[3]
    q_count = q_values.shape[0]
    within = jnp.arange(row_width, dtype=jnp.int32)
    places = (first_b + within[None, :] + q_values[:, None]) % mesh_side
    chosen_bands = jnp.take(col_bands, places, axis=1)
    chosen_pairs = jnp.take(col_pairs, places, axis=1)
    left_pair = (
        row_bands[:, None, :, :band_half, None, :] * chosen_bands[:, :, :, None, :band_half, :]
    )
    right_pair = (
        row_bands[:, None, :, band_half:, None, :] * chosen_bands[:, :, :, None, band_half:, :]
    )
    mixed_pair = jnp.einsum(
        "tqmg,qgh->tqmh",
        left_pair.reshape(line_count, q_count, row_width * band_half * band_half, fourier),
        blocks,
        preferred_element_type=jnp.float32,
    ).astype(jnp.bfloat16)
    mixed_pair = mixed_pair.reshape(line_count, q_count, row_width, band_half, band_half, fourier)
    direct = jnp.einsum(
        "tqiach,tqivwh->tqivawc", mixed_pair, right_pair, preferred_element_type=jnp.float32
    )
    direct = direct.reshape(
        line_count, q_count, row_width, band_half * band_half, band_half * band_half
    )
    scaled = (row_pairs.astype(jnp.float32) * coulomb).astype(jnp.bfloat16)
    exchange_term = jnp.einsum(
        "tisg,tqiug->tqisu", scaled, chosen_pairs, preferred_element_type=jnp.float32
    )
    kernel = 2.0 * exchange_term - direct
    row_place = row_lines[:, None] * mesh_side + first_b + within[None, :]
    col_place = col_lines[:, None, None] * mesh_side + places[None, :, :]
    kept = (col_place >= row_place[:, None, :]) & (kept_mask[:, None, :] > 0)
    kernel = jnp.where(kept[..., None, None], kernel, 0.0)
    chosen_trial = jnp.take(col_trial, places, axis=2)
    row_part = jnp.einsum("tqisu,utqi->sti", kernel, chosen_trial, precision=HIGHEST_PRECISION)
    strict = col_place > row_place[:, None, :]
    col_each = jnp.einsum(
        "tqisu,sti->utqi",
        jnp.where(strict[..., None, None], kernel, 0.0),
        row_trial,
        precision=HIGHEST_PRECISION,
    )
    onehot = (places[:, :, None] == jnp.arange(mesh_side, dtype=jnp.int32)[None, None, :]).astype(
        jnp.float32
    )
    col_part = jnp.einsum("utqi,qic->utc", col_each, onehot, precision=HIGHEST_PRECISION)
    return (row_part, col_part)


def add_into(total, part, start):
    piece = lax.dynamic_slice_in_dim(total, start, part.shape[1], 1)
    return lax.dynamic_update_slice_in_dim(total, piece + part, start, 1)


def local(band_factors, pair_density, screened, coulomb, window_mask, trial_vector):
    col_count = lax.axis_size("col")
    col_index = lax.axis_index("col")
    row_index = lax.axis_index("row")
    midway = col_count // 2
    band_lines, mesh_side = (band_factors.shape[0], band_factors.shape[1])
    row_width = window_mask.shape[1]
    first_b = row_index * row_width
    picked = (
        lax.dynamic_slice_in_dim(band_factors, first_b, row_width, 1),
        lax.dynamic_slice_in_dim(pair_density, first_b, row_width, 1),
        lax.dynamic_slice_in_dim(trial_vector, first_b, row_width, 2),
    )
    row_bands, row_pairs, row_trial = (
        broadcast(picked[0], "col", midway),
        broadcast(picked[1], "col", midway),
        broadcast(picked[2], "col", midway),
    )
    row_trial = row_trial.astype(jnp.float32)
    panel_first = band_lines * midway
    all_q = jnp.arange(mesh_side, dtype=jnp.int32)

    def compute_slab(
        row_start,
        col_start,
        line_count,
        col_band_first,
        col_bands,
        col_pairs,
        col_trial,
        blocks,
        q_values,
    ):
        row_lines = panel_first + row_start + jnp.arange(line_count, dtype=jnp.int32)
        col_lines = col_band_first + col_start + jnp.arange(line_count, dtype=jnp.int32)
        mask_rows = lax.dynamic_slice_in_dim(window_mask, row_start, line_count, 0)
        line_index = jnp.broadcast_to(
            (col_lines % mesh_side)[:, None, None], (line_count, row_width, 1)
        )
        kept_mask = jnp.take_along_axis(mask_rows, line_index, axis=2)[:, :, 0]
        return slab_terms(
            lax.dynamic_slice_in_dim(row_bands, row_start, line_count, 0),
            lax.dynamic_slice_in_dim(row_pairs, row_start, line_count, 0),
            lax.dynamic_slice_in_dim(row_trial, row_start, line_count, 1),
            row_lines,
            first_b,
            lax.dynamic_slice_in_dim(col_bands, col_start, line_count, 0),
            lax.dynamic_slice_in_dim(col_pairs, col_start, line_count, 0),
            lax.dynamic_slice_in_dim(col_trial, col_start, line_count, 1),
            col_lines,
            blocks,
            q_values,
            kept_mask,
            coulomb,
        )

    is_live = col_index >= midway
    live_flag = is_live.astype(jnp.int32)
    received = shifted((band_factors, pair_density, trial_vector), "col", -midway)
    col_bands = jnp.where(is_live, band_factors, received[0])
    col_pairs = jnp.where(is_live, pair_density, received[1])
    col_trial = jnp.where(is_live, trial_vector, received[2]).astype(jnp.float32)
    col_band_first = jnp.where(is_live, col_index, col_index + midway) * band_lines
    center = shifted(screened[0, mesh_side // 2 :], "col", midway)
    blocks = jnp.where(is_live, center, screened[0, : mesh_side // 2])
    q_values = all_q[: mesh_side // 2] + live_flag * (mesh_side // 2)
    row_part, col_part = compute_slab(
        0, 0, band_lines, col_band_first, col_bands, col_pairs, col_trial, blocks, q_values
    )
    row_total = row_part
    col_total = col_part
    below_rows = shifted(screened[1:], "col", midway + 1)
    for line_gap in range(1, band_lines):
        blocks = jnp.where(is_live, below_rows[band_lines - 1 - line_gap], screened[line_gap])
        row_start = live_flag * line_gap
        col_start = (1 - live_flag) * line_gap
        row_part, col_part = compute_slab(
            row_start,
            col_start,
            band_lines - line_gap,
            col_band_first,
            col_bands,
            col_pairs,
            col_trial,
            blocks,
            all_q,
        )
        row_total = add_into(row_total, row_part, row_start)
        col_total = add_into(col_total, col_part, col_start)
    returned = shifted(col_total, "col", midway)
    col_total = jnp.where(is_live, col_total + returned, 0.0)
    row_image = lax.psum_scatter(row_total, "col", scatter_dimension=0, tiled=True)
    col_image = lax.psum_scatter(col_total, "row", scatter_dimension=2, tiled=True)
    return (row_image, col_image)


def solution(mesh):
    placed = (
        P("col", None, None, None),
        P("col", None, None, None),
        P("col", None, None, None),
        P(),
        P(None, "row", None),
        P(None, "col", None),
    )
    return jax.shard_map(
        local,
        mesh=mesh,
        in_specs=placed,
        out_specs=(P("col", None, "row"), P(None, "col", "row")),
        check_vma=False,
    )
```

profile of v0, /device:TPU:1, one launch (start us, length us, event | category | flops | bytes accessed | tf_op | source)
XLA Modules:
  0.0 798.2 jit_solution(10363889306173101909)
XLA Ops:
  8.5 10.6 %slice.69 = bf16[2,48,256,256]{3,2,1,0:T(8,128)(2,1)} slice(bf16[3,48,256,256]{3,2,1,0:T(8,128)(2,1)} %param.8), slice={[1:3], [0:48], [0:256], [0:256]} | slice | bytes 25165824 | tf_op jit(solution)/shard_map/slice | solution.py:164
  19.1 13.2 %collective-permute-start.4 = (bf16[2,48,256,256]{3,2,1,0:T(8,128)(2,1)}, bf16[2,48,256,256]{3,2,1,0:T(8,128)(2,1)}, u32[]{:S(2)}, u32[]{:S(2)}) collective-permute-start(bf16[2,48,256,256]{3,2,1,0:T(8,128)(2,1)} %slice.69), channel_id=1, source_target_pairs={{0,9},{1,10},{2,11},{3,12},{4,13},{5,14},{6,15},{16,25},{17,26},{1... | collective-permute-start | bytes 37748744 | tf_op jit(solution)/shard_map/ppermute | solution.py:17
  38.9 8.3 %collective-permute-start.3 = (bf16[24,256,256]{2,1,0:T(8,128)(2,1)}, bf16[24,256,256]{2,1,0:T(8,128)(2,1)}, u32[]{:S(2)}, u32[]{:S(2)}) collective-permute-start(bf16[24,256,256]{2,1,0:T(8,128)(2,1)} %slice_bitcast_fusion), channel_id=1, source_target_pairs={{0,8},{1,9},{2,10},{3,11},{4,12},{5,13},{6,14},{7,15},{16,24},{17,... | collective-permute-start | bytes 9437192 | tf_op jit(solution)/shard_map/ppermute | solution.py:17
  53.1 327.6 %psum.23 = bf16[16,3,6]{0,2,1:T(8,128)(2,1)S(1)} all-reduce(bf16[16,3,6]{0,2,1:T(8,128)(2,1)S(1)} %broadcast_select_fusion.4), channel_id=1, replica_groups=mesh['row'=8,'col'=16] {'col'}, use_global_device_ids=true, to_apply=%region_3.4 | all-reduce | flops 288 | bytes 1152 | tf_op jit(solution)/shard_map/psum | solution.py:11
  394.6 37.4 %all-reduce.5.cloned.1.call-done = (bf16[3,6,8,256]{3,2,1,0:T(8,128)(2,1)}, bf16[3,6,16,256]{3,2,1,0:T(8,128)(2,1)}) async-done(((bf16[3,6,8,256]{3,2,1,0:T(8,128)(2,1)}, bf16[3,6,16,256]{3,2,1,0:T(8,128)(2,1)}), (bf16[3,6,8,256]{3,2,1,0:T(8,128)(2,1)}, bf16[3,6,16,256]{3,2,1,0:T(8,128)(2,1)})) %all-reduce.5.cloned.1.call-update) | async-done | bytes 221200 | tf_op jit(solution)/shard_map/psum | solution.py:11
  448.4 7.8 mul.255
  461.0 6.8 mul.239
  478.4 13.6 %gather_fusion.4 = bf16[288,2,16,256]{3,2,1,0:T(8,128)(2,1)} fusion(bf16[2,48,16,256]{3,2,1,0:T(8,128)(2,1)S(1)} %constant_dynamic-slice_fusion.8, s32[1024]{0:T(1024)S(1)} %pad_clamp_fusion), kind=kCustom, calls=%fused_computation.4 | custom fusion | bytes 9438336 | tf_op jit(solution)/shard_map/jit(_take)/gather | solution.py:43
  495.0 6.2 convert_bitcast_fusion.1
  501.2 5.7 reshape.941
  506.9 20.6 %convolution_bitcast_fusion.1 = f32[3,24,6,4,4,4,4]{6,5,4,3,2,1,0:T(4,128)} fusion(bf16[3,6,4,256]{3,2,1,0:T(4,128)(2,1)} %get-tuple-element.20, bf16[3,24,6,4,4,256]{5,4,3,2,0,1:T(4,128)(2,1)S(1)} %reshape.941, bf16[3,24,6,4,256]{4,3,0,2,1:T(4,128)(2,1)} %get-tuple-element.12), kind=kOutput, calls=%fused_computation.13 | convolution fusion | flops 63700992 | bytes 4902912 | tf_op jit(solution)/shard_map/tqiach,tqivwh->tqivawc/dot_general | solution.py:57
  527.5 13.2 %copy.66 = f32[3,24,6,4,4,4,4]{1,6,5,4,3,2,0:T(4,128)S(1)} copy(f32[3,24,6,4,4,4,4]{6,5,4,3,2,1,0:T(4,128)} %convolution_bitcast_fusion.1) | data formatting | bytes 884736 | tf_op jit(solution)/shard_map/tqiach,tqivwh->tqivawc/transpose | solution.py:57
  547.8 13.7 %fusion.23 = f32[3,6,1,24,16]{4,2,3,1,0:T(1,128)} fusion(f32[3,24,6,16,16]{3,4,1,2,0:T(8,128)S(1)} %fusion.20, pred[3,24,6]{1,2,0:T(8,128)(4,1)S(1)} %copy-done.23, bf16[16,3,6,1,1]{0,2,1,3,4:T(8,128)(2,1)S(1)} %bitcast.283), kind=kOutput, calls=%fused_computation.45 | convolution fusion | flops 1437696 | bytes 471024 | tf_op jit(solution)/shard_map/tqisu,sti->utqi/dot_general | solution.py:75
  567.5 9.1 %convert_bitcast_fusion = bf16[2,48,96,256]{3,2,0,1:T(8,128)(2,1)} fusion(bf16[2,48,96,256]{3,2,0,1:T(8,128)(2,1)} %mul.255, bf16[2,48,256,256]{3,2,1,0:T(8,128)(2,1)} %collective-permute-done.4, bf16[3,48,256,256]{3,2,1,0:T(8,128)(2,1)} %param.8, pred[]{:T(512)S(6)} %ge.124, bf16[2,96,256]{2,1,0:T(8,128)(2,1)S(1)} %copy-done.13), kind=kOutput, calls=%fused_computation.34 | convolution fusion | flops 1222901760 | bytes 22118400 | tf_op jit(solution)/shard_map/tqmg,qgh->tqmh/dot_general | solution.py:50
  576.6 7.8 reshape.943
  584.4 46.0 %convolution_bitcast_fusion = f32[2,48,6,4,4,4,4]{6,5,4,3,2,1,0:T(4,128)} fusion(bf16[2,6,4,256]{3,2,1,0:T(4,128)(2,1)S(1)} %copy-done.21, bf16[2,48,6,4,4,256]{5,4,3,2,0,1:T(4,128)(2,1)} %reshape.943, bf16[2,48,6,4,256]{4,3,0,2,1:T(4,128)(2,1)S(1)} %copy-done.5), kind=kOutput, calls=%fused_computation.12 | convolution fusion | flops 84934656 | bytes 6512640 | tf_op jit(solution)/shard_map/tqiach,tqivwh->tqivawc/dot_general | solution.py:57
  630.4 15.6 %copy.75 = f32[2,48,6,4,4,4,4]{1,6,5,4,3,2,0:T(4,128)S(1)} copy(f32[2,48,6,4,4,4,4]{6,5,4,3,2,1,0:T(4,128)} %convolution_bitcast_fusion) | data formatting | bytes 1179648 | tf_op jit(solution)/shard_map/tqiach,tqivwh->tqivawc/transpose | solution.py:57
  649.5 5.9 multiply_reduce_fusion.1
  657.9 8.2 %convert_bitcast_fusion.2 = bf16[1,48,96,256]{3,2,1,0:T(8,128)(2,1)} fusion(bf16[2,48,256,256]{3,2,1,0:T(8,128)(2,1)} %collective-permute-done.4, bf16[3,48,256,256]{3,2,1,0:T(8,128)(2,1)} %param.8, pred[]{:T(512)S(6)} %ge.124, bf16[48,96,256]{2,1,0:T(8,128)(2,1)S(1)} %copy-done.4, bf16[96,256]{1,0:T(8,128)(2,1)S(1)} %copy-done.16), kind=kOutput, calls=%fused_computation.69 | convolution fusion | flops 613023744 | bytes 17350656 | tf_op jit(solution)/shard_map/tqmg,qgh->tqmh/dot_general | solution.py:50
  670.3 12.8 %convolution_bitcast_fusion.2 = f32[1,48,6,4,4,4,4]{6,5,4,3,2,1,0:T(4,128)} fusion(bf16[48,6,4,4,256,1]{4,3,2,1,0,5:T(4,128)(2,1)S(1)} %reshape.1099, bf16[48,6,4,256]{3,2,1,0:T(4,128)(2,1)S(1)} %copy-done.8, bf16[6,4,256]{2,1,0:T(4,128)(2,1)S(1)} %copy-done.24), kind=kOutput, calls=%fused_computation.24 | convolution fusion | flops 42467328 | bytes 3256320 | tf_op jit(solution)/shard_map/tqiach,tqivwh->tqivawc/dot_general | solution.py:57
  683.1 8.2 %copy.82 = f32[1,48,6,4,4,4,4]{1,6,5,4,3,2,0:T(4,128)S(1)} copy(f32[1,48,6,4,4,4,4]{6,5,4,3,2,1,0:T(4,128)} %convolution_bitcast_fusion.2) | data formatting | bytes 589824 | tf_op jit(solution)/shard_map/tqiach,tqivwh->tqivawc/transpose | solution.py:57
  693.7 4.4 fusion.43
  701.4 52.1 %all-reduce = f32[16,3,6]{2,1,0:T(4,128)S(1)} all-reduce(f32[16,3,6]{2,1,0:T(4,128)S(1)} %copy.84), channel_id=2, replica_groups=mesh['row'=8,'col'=16] {'col'}, use_global_device_ids=true, to_apply=%region_2.3.clone | all-reduce | flops 288 | bytes 2304
  754.9 35.6 %all-reduce.1 = f32[16,3,48]{0,1,2:T(4,128)S(1)} all-reduce(f32[16,3,48]{0,1,2:T(4,128)S(1)} %copy.87), channel_id=3, replica_groups=mesh['row'=8,'col'=16] {'row'}, use_global_device_ids=true, to_apply=%region_4.5.clone | all-reduce | flops 2304 | bytes 18432
  (220 shorter events, 92.1 us)
Async XLA Ops:
  7.2 42.8 %copy-start = (s32[3,6,48]{2,1,0:T(8,128)S(1)}, s32[3,6,48]{2,1,0:T(8,128)}, u32[]{:S(2)}) copy-start(s32[3,6,48]{2,1,0:T(8,128)} %param.10) | copy-start | bytes 10372
  7.2 25.1 %copy-start.17 = (bf16[16,3,48]{2,0,1:T(8,128)(2,1)S(1)}, bf16[16,3,48]{2,0,1:T(8,128)(2,1)}, u32[]{:S(2)}) copy-start(bf16[16,3,48]{2,0,1:T(8,128)(2,1)} %param.11) | copy-start | bytes 13828
  7.2 424.8 %all-reduce.5.cloned.1.call-start = ((), (), s32[]{:S(2)}) async-start(), calls=%async_computation | async-start | bytes 442368 | tf_op jit(solution)/shard_map/psum | solution.py:11
  7.2 430.8 %collective-permute-start.2 = (bf16[3,48,8,256]{3,2,1,0:T(8,128)(2,1)}, bf16[3,48,8,256]{3,2,1,0:T(8,128)(2,1)S(1)}, u32[]{:S(2)}, u32[]{:S(2)}) collective-permute-start(bf16[3,48,8,256]{3,2,1,0:T(8,128)(2,1)} %param.6), channel_id=1, source_target_pairs={{8,0},{9,1},{10,2},{11,3},{12,4},{13,5},{14,6},{15,7},{24,16},{25,... | collective-permute-start | bytes 1769480 | tf_op jit(solution)/shard_map/ppermute | solution.py:17
  19.1 29.7 %copy-start.6 = (bf16[3,48,8,256]{3,2,1,0:T(8,128)(2,1)S(1)}, bf16[3,48,8,256]{3,2,1,0:T(8,128)(2,1)}, u32[]{:S(2)}) copy-start(bf16[3,48,8,256]{3,2,1,0:T(8,128)(2,1)} %param.6) | copy-start | bytes 1769476
  19.1 548.4 %collective-permute-start.4 = (bf16[2,48,256,256]{3,2,1,0:T(8,128)(2,1)}, bf16[2,48,256,256]{3,2,1,0:T(8,128)(2,1)}, u32[]{:S(2)}, u32[]{:S(2)}) collective-permute-start(bf16[2,48,256,256]{3,2,1,0:T(8,128)(2,1)} %slice.69), channel_id=1, source_target_pairs={{0,9},{1,10},{2,11},{3,12},{4,13},{5,14},{6,15},{16,25},{17,26},{1... | collective-permute-start | bytes 37748744 | tf_op jit(solution)/shard_map/ppermute | solution.py:17
  32.3 354.9 %collective-permute-start = (bf16[16,3,48]{2,0,1:T(8,128)(2,1)S(1)}, bf16[16,3,48]{2,0,1:T(8,128)(2,1)S(1)}, u32[]{:S(2)}, u32[]{:S(2)}) collective-permute-start(bf16[16,3,48]{2,0,1:T(8,128)(2,1)S(1)} %copy-done.17), channel_id=1, source_target_pairs={{8,0},{9,1},{10,2},{11,3},{12,4},{13,5},{14,6},{15,7},{24,16},{25,... | collective-permute-start | bytes 13832 | tf_op jit(solution)/shard_map/ppermute | solution.py:17
  33.6 440.5 %collective-permute-start.1 = (bf16[3,48,16,256]{3,2,1,0:T(8,128)(2,1)}, bf16[3,48,16,256]{3,2,1,0:T(8,128)(2,1)}, u32[]{:S(2)}, u32[]{:S(2)}) collective-permute-start(bf16[3,48,16,256]{3,2,1,0:T(8,128)(2,1)} %param.7), channel_id=1, source_target_pairs={{8,0},{9,1},{10,2},{11,3},{12,4},{13,5},{14,6},{15,7},{24,16},{25,... | collective-permute-start | bytes 3538952 | tf_op jit(solution)/shard_map/ppermute | solution.py:17
  38.9 346.4 %copy-start.35 = (u32[128]{0:T(128)S(1)}, u32[128]{0:T(128)}, u32[]{:S(2)}) copy-start(u32[128]{0:T(128)} %constant.311) | copy-start | bytes 1540
  38.9 347.0 %copy-start.34 = (u32[128]{0:T(128)S(1)}, u32[128]{0:T(128)}, u32[]{:S(2)}) copy-start(u32[128]{0:T(128)} %constant.307) | copy-start | bytes 1540
  38.9 456.1 %collective-permute-start.3 = (bf16[24,256,256]{2,1,0:T(8,128)(2,1)}, bf16[24,256,256]{2,1,0:T(8,128)(2,1)}, u32[]{:S(2)}, u32[]{:S(2)}) collective-permute-start(bf16[24,256,256]{2,1,0:T(8,128)(2,1)} %slice_bitcast_fusion), channel_id=1, source_target_pairs={{0,8},{1,9},{2,10},{3,11},{4,12},{5,13},{6,14},{7,15},{16,24},{17,... | collective-permute-start | bytes 9437192 | tf_op jit(solution)/shard_map/ppermute | solution.py:17
  52.5 339.7 %copy-start.18 = (s32[24,6]{0,1:T(8,128)}, s32[24,6]{0,1:T(8,128)S(1)}, u32[]{:S(2)}) copy-start(s32[24,6]{0,1:T(8,128)S(1)} %copy.60) | copy-start | bytes 1732
  383.2 9.0 %copy-start.27 = (pred[48,6]{0,1:T(8,128)(4,1)}, pred[48,6]{0,1:T(8,128)(4,1)S(1)}, u32[]{:S(2)}) copy-start(pred[48,6]{0,1:T(8,128)(4,1)S(1)} %get-tuple-element.30) | copy-start | bytes 868
  384.7 84.9 %copy-start.10 = (pred[48,6]{1,0:T(8,128)(4,1)}, pred[48,6]{1,0:T(8,128)(4,1)S(1)}, u32[]{:S(2)}) copy-start(pred[48,6]{1,0:T(8,128)(4,1)S(1)} %copy.68) | copy-start | bytes 868
  448.4 7.8 copy-start.2
  547.8 19.4 %copy-start.19 = (s32[24,6]{0,1:T(8,128)S(1)}, s32[24,6]{0,1:T(8,128)}, u32[]{:S(2)}) copy-start(s32[24,6]{0,1:T(8,128)} %copy-done.18) | copy-start | bytes 1732
  576.6 7.8 copy-start.5
  576.6 7.8 copy-start.21
  683.1 10.6 %copy-start.3 = (bf16[288,16,256]{2,1,0:T(8,128)(2,1)S(1)}, bf16[288,16,256]{2,1,0:T(8,128)(2,1)}, u32[]{:S(2)}) copy-start(bf16[288,16,256]{2,1,0:T(8,128)(2,1)} %gather_fusion.7) | copy-start | bytes 7077892
  683.1 10.6 %copy-start.11 = (pred[48,6]{1,0:T(8,128)(4,1)S(1)}, pred[48,6]{1,0:T(8,128)(4,1)}, u32[]{:S(2)}) copy-start(pred[48,6]{1,0:T(8,128)(4,1)} %copy-done.10) | copy-start | bytes 868
  683.1 10.6 %copy-start.12 = (f32[6,48,16]{2,1,0:T(8,128)S(1)}, f32[6,48,16]{2,1,0:T(8,128)}, u32[]{:S(2)}) copy-start(f32[6,48,16]{2,1,0:T(8,128)} %copy.144) | copy-start | bytes 55300
  683.1 10.6 %copy-start.31 = (pred[48,6]{0,1:T(8,128)(4,1)S(1)}, pred[48,6]{0,1:T(8,128)(4,1)}, u32[]{:S(2)}) copy-start(pred[48,6]{0,1:T(8,128)(4,1)} %get-tuple-element.29) | copy-start | bytes 868
  693.7 97.4 %copy-start.1 = (s32[3,6,48]{2,1,0:T(8,128)S(1)}, s32[3,6,48]{2,1,0:T(8,128)}, u32[]{:S(2)}) copy-start(s32[3,6,48]{2,1,0:T(8,128)} %param.10) | copy-start | bytes 10372
  700.0 54.8 %collective-permute-start.5 = (f32[16,3,48]{2,0,1:T(8,128)S(1)}, f32[16,3,48]{2,0,1:T(8,128)S(1)}, u32[]{:S(2)}, u32[]{:S(2)}) collective-permute-start(f32[16,3,48]{2,0,1:T(8,128)S(1)} %fusion.75), channel_id=1, source_target_pairs={{0,8},{1,9},{2,10},{3,11},{4,12},{5,13},{6,14},{7,15},{16,24},{17,... | collective-permute-start | bytes 27656 | tf_op jit(solution)/shard_map/ppermute | solution.py:17
  (19 other events, 73.9 us)
Sparse Core Ops, SparseCore 0:
  49.6 382.3 all-reduce.4
where the time goes:
time: 813 us; the launch traced here: 798 us
  blocking collectives  415 us (51%)
  local copies, waits for them, and re-layouts  153 us (19%)
  matrix products  136 us (17%)
  waiting for transfers between devices  37.4 us (5%)
  starting transfers between devices  26.8 us (3%)
  between operations  15.8 us (2%)
  other arithmetic  14 us (2%)
    psum x1, blocking collectives, broadcast(): return lax.psum(block, axis)  328 us
    unnamed x2, blocking collectives  87.7 us
    dot_general x3, matrix products, slab_terms(): jnp.einsum('tqiach,tqivwh->tqivawc', mixed_pair, right_pair, preferred_el...  79.3 us
    psum x1, waiting for transfers between devices, broadcast(): return lax.psum(block, axis)  37.4 us
    transpose x3, local copies, waits for them, and re-layouts, slab_terms(): jnp.einsum('tqiach,tqivwh->tqivawc', mixed_pair, right_pair, preferred_el...  37 us
    ppermute x6, starting transfers between devices, shifted(): return lax.ppermute(block, axis, route)  26.7 us
    mul x12, local copies, waits for them, and re-layouts, slab_terms(): row_bands[:, None, :, :band_half, None, :]  24.9 us
    dot_general x3, matrix products, slab_terms(): jnp.einsum('tqmg,qgh->tqmh', left_pair.reshape(line_count, q_count, row_w...  23.5 us
  transfers between devices with their start and end apart: 7, of which 1 were waited for; matrix products, arithmetic and copies ran while one was open for 21% of the time, Pallas kernels for 0%

commit v1 on v0

v1 whole, which is shorter than its diff:
```python
import functools

import jax
import jax.numpy as jnp
from jax import lax
from jax.experimental import pallas as pl
from jax.experimental.pallas import tpu as pltpu
from jax.sharding import PartitionSpec as P

MESH = pl.DeviceIdType.MESH
F32 = jnp.float32
BF16 = jnp.bfloat16
SIDE = 48
ROWS = 8
WIDTH = 6
LINES = 3
HALF = 8
SLOTS = 2 * LINES - 1
RING = SIDE + 8
Q_STEP = 4
HIGHEST = lax.Precision.HIGHEST
ANY = pl.BlockSpec(memory_space=pl.ANY)
VMEM = pl.BlockSpec(memory_space=pltpu.VMEM)


def iota(shape, axis):
    return lax.broadcasted_iota(jnp.int32, shape, axis)


def dot(a, b, contract=(1, 0), precision=None):
    return lax.dot_general(
        a,
        b,
        (((contract[0],), (contract[1],)), ((), ())),
        preferred_element_type=F32,
        precision=precision,
    )


def ones_where(condition, dtype=BF16):
    return jnp.where(condition, 1.0, 0.0).astype(dtype)


def block_diagonal(trial_line, first, copies):
    pick = ones_where(iota((8, SIDE), 1) == first + iota((8, SIDE), 0))
    rows = dot(pick, trial_line).astype(BF16)
    tiled = dot(rows, ones_where(iota((16, copies * 16), 1) % 16 == iota((16, copies * 16), 0)))
    return jnp.where(iota(tiled.shape, 1) // 16 == iota(tiled.shape, 0), tiled, 0.0)


def greet():
    row, col = lax.axis_index("row"), lax.axis_index("col")
    barrier = pltpu.get_barrier_semaphore()
    for step in range(1, ROWS):
        pl.semaphore_signal(
            barrier, inc=1, device_id=(lax.rem(row + step, ROWS), col), device_id_type=MESH
        )
    for step in range(1, 2 * HALF):
        pl.semaphore_signal(
            barrier, inc=1, device_id=(row, lax.rem(col + step, 2 * HALF)), device_id_type=MESH
        )
    pl.semaphore_wait(barrier, ROWS + 2 * HALF - 2)


def remote(source, target, send_sem, recv_sem, device):
    return pltpu.make_async_remote_copy(
        src_ref=source,
        dst_ref=target,
        send_sem=send_sem,
        recv_sem=recv_sem,
        device_id=device,
        device_id_type=MESH,
    )


def gather_kernel(
    bands,
    density,
    trial,
    window,
    trial_v,
    coulomb,
    panel,
    masks,
    cols,
    ctrial,
    ptrial,
    rvec,
    dens_v,
    rsend,
    send,
    recv,
    local,
):
    row, col = lax.axis_index("row"), lax.axis_index("col")
    first = row * WIDTH
    greet()
    own = bands.at[:, pl.ds(first, WIDTH)]

    def to(source, target, number, arrives, device):
        return remote(source, target, send.at[number], recv.at[arrives], device)

    def column_copies():
        near = (row, lax.rem(col + HALF, 2 * HALF))
        return [
            to(own, cols.at[0:LINES], 8, 0, near),
            to(trial, ctrial.at[0], 9, 2, near),
        ]

    def next_copies():
        far = (row, lax.rem(col + HALF - 1, 2 * HALF))
        return [
            to(bands.at[0 : LINES - 1, pl.ds(first, WIDTH)], cols.at[LINES:SLOTS], 10, 1, far),
            to(trial, ctrial.at[1], 11, 3, far),
        ]

    def panel_copies():
        return [to(own, panel.at[row], j, 5, (row, j)) for j in range(HALF)] + [
            to(trial, ptrial, 16 + j, 4, (row, j)) for j in range(HALF)
        ]

    def vector_copies():
        return [to(rsend, rvec, 24 + j, 6, (row, HALF + j)) for j in range(1, HALF)]

    def row_copies():
        copies = []
        for step in range(1, ROWS):
            peer = lax.rem(row + step, ROWS)
            copies.append(to(panel.at[row], panel.at[row], step, 8 + step, (peer, col)))
        return copies

    def mask_copies():
        copies = []
        for step in range(1, ROWS):
            peer = lax.rem(row + step, ROWS)
            copies.append(to(window, masks.at[row], 8 + step, 16 + step, (peer, col)))
        return copies

    @pl.when(col < HALF)
    def _():
        keep = pltpu.make_async_copy(window, masks.at[row], local.at[0])
        keep.start()
        for copy in mask_copies():
            copy.start()
        to(own, panel.at[row], 0, 5, (row, HALF)).wait_recv()
        for copy in row_copies():
            copy.start()
        to(own, cols.at[0:LINES], 0, 0, (row, HALF)).wait_recv()
        to(trial, ctrial.at[0], 0, 2, (row, HALF)).wait_recv()
        to(trial, ptrial, 0, 4, (row, HALF)).wait_recv()

        @pl.when(col < HALF - 1)
        def _():
            to(cols.at[LINES:SLOTS], cols.at[LINES:SLOTS], 0, 1, (row, HALF)).wait_recv()
            to(trial, ctrial.at[1], 0, 3, (row, HALF)).wait_recv()

        for step in range(1, ROWS):
            source = lax.rem(row + ROWS - step, ROWS)
            to(panel.at[source], panel.at[source], 0, 8 + step, (source, col)).wait_recv()
            to(window, masks.at[source], 0, 16 + step, (source, col)).wait_recv()
        for copy in row_copies():
            copy.wait_send()
        for copy in mask_copies():
            copy.wait_send()
        keep.wait()

    @pl.when(col >= HALF)
    def _():
        @pl.when(col == HALF)
        def _():
            fetch = pltpu.make_async_copy(density.at[:, pl.ds(first, WIDTH)], dens_v, local.at[0])
            fetch.start()
            for copy in panel_copies():
                copy.start()
            fetch.wait()
            for t in range(LINES):
                diagonal = block_diagonal(trial_v[t], first, WIDTH).astype(BF16)
                scaled = (dens_v[t].astype(F32) * coulomb[...]).astype(BF16)
                rsend[t] = dot(diagonal, scaled.reshape(WIDTH * 16, 256))
            for copy in vector_copies():
                copy.start()
            keep = pltpu.make_async_copy(rsend, rvec, local.at[1])
            keep.start()
            keep.wait()

        for copy in column_copies():
            copy.start()

        @pl.when(col > HALF)
        def _():
            for copy in next_copies():
                copy.start()
            to(rsend, rvec, 0, 6, (row, HALF)).wait_recv()
            for copy in next_copies():
                copy.wait_send()

        for copy in column_copies():
            copy.wait_send()

        @pl.when(col == HALF)
        def _():
            for copy in panel_copies():
                copy.wait_send()
            for copy in vector_copies():
                copy.wait_send()


def gather(bands, density, trial, window, coulomb):
    shapes = [
        jax.ShapeDtypeStruct((ROWS, LINES, WIDTH, 8, 256), BF16),
        jax.ShapeDtypeStruct((ROWS, LINES, WIDTH, SIDE), jnp.int32),
        jax.ShapeDtypeStruct((SLOTS, WIDTH, 8, 256), BF16),
        jax.ShapeDtypeStruct((2, LINES, SIDE, 16), BF16),
        jax.ShapeDtypeStruct((LINES, SIDE, 16), BF16),
        jax.ShapeDtypeStruct((LINES, 8, 256), F32),
    ]
    return pl.pallas_call(
        gather_kernel,
        name="gather",
        out_shape=shapes,
        in_specs=[ANY, ANY, ANY, ANY, VMEM, VMEM],
        out_specs=[ANY] * len(shapes),
        scratch_shapes=[
            pltpu.VMEM((LINES, WIDTH, 16, 256), BF16),
            pltpu.VMEM((LINES, 8, 256), F32),
            pltpu.SemaphoreType.DMA((32,)),
            pltpu.SemaphoreType.DMA((24,)),
            pltpu.SemaphoreType.DMA((2,)),
        ],
        compiler_params=pltpu.CompilerParams(collective_id=0, has_side_effects=True),
    )(bands, density, trial, window, trial, coulomb)


def pair_kernel(
    blocks,
    panel,
    masks,
    cols,
    ctrial,
    ptrial,
    density,
    rvec,
    trial,
    window,
    zrow,
    zcol,
    pvec,
    zex,
    flat,
    left_t,
    y_row,
    keep_t,
    r_sum,
    col_flat,
    u_col,
    y_col,
    c_sum,
):
    row, col = lax.axis_index("row"), lax.axis_index("col")
    step = pl.program_id(0)
    first = row * WIDTH
    halves = (slice(0, 128), slice(128, 256))
    spread = ones_where(iota((16, 2048), 1) // 128 == iota((16, 2048), 0))

    def lane(expanded, s):
        return expanded[:, s * 128 : (s + 1) * 128]

    def store_ring(table, h, number, value):
        base = number * RING
        table[h, base : base + SIDE, :] = value
        table[h, base + SIDE : base + RING, :] = value[0:8]

    def prepare_panel():
        for t in range(LINES):
            for source in range(ROWS):
                value = panel[source, t].astype(F32).reshape(SIDE, 256)
                base = (t * ROWS + source) * SIDE
                for h in range(2):
                    flat[h, base : base + SIDE, :] = value[:, halves[h]]
        for t in range(LINES):
            expanded = dot(ptrial[t], spread)
            for h in range(2):

                def band(number):
                    return flat[h, pl.ds(t * 8 * SIDE + number, SIDE, stride=8), :]

                for c in range(4):
                    store_ring(left_t, h, t * 4 + c, band(c))
                valence = [band(4 + v) for v in range(4)]
                for c in range(4):
                    total = valence[0] * lane(expanded, c)
                    for v in range(1, 4):
                        total += valence[v] * lane(expanded, 4 * v + c)
                    store_ring(y_row, h, t * 4 + c, total)
        places = iota((WIDTH, SIDE), 1)
        for t in range(LINES):
            for e in range(LINES):
                line = HALF * LINES + t + col * LINES + e
                base = (e * LINES + t) * RING
                for source in range(ROWS):
                    held = jnp.where(places == line, masks[source, t], 0).astype(F32)
                    factor = jnp.broadcast_to(jnp.sum(held, axis=1, keepdims=True), (WIDTH, 128))
                    keep_t[base + source * WIDTH : base + (source + 1) * WIDTH, :] = factor
                keep_t[base + SIDE : base + RING, :] = keep_t[base : base + 8, :]
        r_sum[...] = jnp.zeros_like(r_sum)

    def prepare_columns():
        col_flat[...] = jnp.zeros_like(col_flat)
        for a in range(SLOTS):
            value = cols[a].astype(F32).reshape(WIDTH * 8, 256)
            if a >= LINES:
                value = jnp.where(col < HALF - 1, value, 0.0)
            for h in range(2):
                col_flat[h, a * 64 : a * 64 + WIDTH * 8, :] = value[:, halves[h]]
        pick = ones_where(iota((8, SIDE), 1) == first + iota((8, SIDE), 0))
        for a in range(SLOTS):
            line = ctrial[a // LINES, a % LINES]
            expanded = dot(dot(pick, line).astype(BF16), spread)
            if a >= LINES:
                expanded = jnp.where(col < HALF - 1, expanded, 0.0)
            for h in range(2):

                def band(number):
                    return col_flat[h, pl.ds(a * 64 + number, 8, stride=8), :]

                for pair in range(2):
                    both = jnp.concatenate([band(2 * pair), band(2 * pair + 1)], axis=0)
                    u_col[a * 32 + pair * 16 : a * 32 + pair * 16 + 16, halves[h]] = both.astype(
                        BF16
                    )
                valence = [band(4 + v) for v in range(4)]
                for c in range(4):
                    total = valence[0] * lane(expanded, c)
                    for v in range(1, 4):
                        total += valence[v] * lane(expanded, 4 * v + c)
                    y_col[h, (a * 4 + c) * 8 : (a * 4 + c) * 8 + 8, :] = total
        c_sum[...] = jnp.zeros_like(c_sum)

    def one_block(qq, carry):
        q_value = step * Q_STEP + qq
        start = lax.rem(first + SIDE - q_value, SIDE)
        inside = (first + iota((8, 128), 0) >= q_value) | (col > 0)
        same = (q_value == 0) & (col == 0)
        for t in range(LINES):

            def rows(table, c, h):
                return table[h, pl.ds((t * 4 + c) * RING + start, 8), :]

            lefts = [[rows(left_t, c, h) for h in range(2)] for c in range(4)]
            backs = [[rows(y_row, c, h) for h in range(2)] for c in range(4)]
            totals = [[None, None] for _ in range(4)]
            for e in range(LINES):
                a = t + e
                factor = keep_t[pl.ds((e * LINES + t) * RING + start, 8), :]
                if e == 0:
                    factor = jnp.where(inside, factor, 0.0)
                tiles = []
                for c in range(4):
                    both = []
                    for h in range(2):
                        kept = lefts[c][h] * factor
                        both.append(jnp.concatenate([kept, kept], axis=0).astype(BF16))
                    both = jnp.concatenate(both, axis=1)
                    for pair in range(2):
                        base = a * 32 + pair * 16
                        tiles.append(both * u_col[base : base + 16, :])
                mixed = dot(jnp.concatenate(tiles, axis=0), blocks[e, qq])
                for h in range(2):
                    images = [None] * 4
                    for c in range(4):
                        for d in range(4):
                            base = (c * 4 + d) * 8
                            piece = mixed[base : base + 8, halves[h]]
                            base = (a * 4 + d) * 8
                            part = piece * y_col[h, base : base + 8, :]
                            totals[c][h] = part if totals[c][h] is None else totals[c][h] + part
                            part = piece * backs[c][h]
                            images[d] = part if images[d] is None else images[d] + part
                    for d in range(4):
                        base = (a * 4 + d) * 8
                        image = jnp.where(same, 0.0, images[d]) if e == 0 else images[d]
                        c_sum[h, base : base + 8, :] += image
            for c in range(4):
                for h in range(2):
                    r_sum[h, pl.ds((t * 4 + c) * RING + start, 8), :] += totals[c][h]
        return carry

    def finish():
        lanes = iota((SIDE, 128), 1)
        image = jnp.zeros((SIDE, 128), F32)
        for t in range(LINES):
            for c in range(4):
                base = (t * 4 + c) * RING
                total = []
                for h in range(2):
                    head = r_sum[h, base : base + 8, :] + r_sum[h, base + SIDE : base + RING, :]
                    total.append(
                        jnp.concatenate([head, r_sum[h, base + 8 : base + SIDE, :]], axis=0)
                    )
                for v in range(4):
                    product = 0.0
                    for h in range(2):
                        strided = pl.ds(t * 8 * SIDE + 4 + v, SIDE, stride=8)
                        product += flat[h, strided, :] * total[h]
                    value = jnp.sum(product, axis=1, keepdims=True)
                    image = jnp.where(lanes == t * 16 + 4 * v + c, value, image)
        for target in range(ROWS):
            zrow[target, 0:WIDTH, :] = -image[target * WIDTH : (target + 1) * WIDTH]
            zrow[target, WIDTH:8, :] = jnp.zeros((8 - WIDTH, 128), F32)
        lanes = iota((8, 128), 1)
        for a in range(SLOTS):
            image = jnp.zeros((8, 128), F32)
            for v in range(4):
                for c in range(4):
                    product = 0.0
                    for h in range(2):
                        base = (a * 4 + c) * 8
                        strided = pl.ds(a * 64 + 4 + v, 8, stride=8)
                        product += col_flat[h, strided, :] * c_sum[h, base : base + 8, :]
                    value = jnp.sum(product, axis=1, keepdims=True)
                    image = jnp.where(lanes == 4 * v + c, value, image)
            zcol[a] = -image

    def exchange():
        tile = ones_where(iota((16, SIDE * 16), 1) % 16 == iota((16, SIDE * 16), 0))
        own_point = iota((SIDE, SIDE * 16), 1) // 16 == iota((SIDE, SIDE * 16), 0)
        ones = jnp.ones((8, SIDE), BF16)
        points = iota((8, SIDE * 16), 1) // 16
        row_points = first + iota((8, SIDE * 16), 0)
        places = iota((WIDTH, SIDE), 1)
        wide = jnp.concatenate([rvec[t] for t in range(LINES)], axis=0)
        high = wide.astype(BF16)
        low = (wide - high.astype(F32)).astype(BF16)
        split = jnp.concatenate([high, low], axis=0)
        zex[...] = jnp.zeros_like(zex)
        sums = jnp.zeros((8 * LINES, 256), F32)
        for a in range(LINES):
            line = col * LINES + a
            values = jnp.where(own_point, dot(trial[a], tile), 0.0).astype(BF16)
            values = dot(ones, values)
            kept_values = []
            strict_factors = []
            for t in range(LINES):
                row_line = HALF * LINES + t
                held = jnp.where(places == line, window[t], 0).astype(F32)
                held = jnp.sum(held, axis=1, keepdims=True)
                held = jnp.concatenate([held, jnp.zeros((8 - WIDTH, 1), F32)], axis=0)
                kept = (line > row_line) | ((line == row_line) & (points >= row_points))
                strict = (line > row_line) | ((line == row_line) & (points > row_points))
                kept_values.append(jnp.where(kept, held, 0.0) * values)
                strict_factors.append(jnp.where(strict, held, 0.0))
            table = density[a].reshape(SIDE * 16, 256)
            sums += dot(jnp.concatenate(kept_values, axis=0).astype(BF16), table)
            products = dot(split, table, (1, 1))
            products = products[0 : 8 * LINES] + products[8 * LINES : 16 * LINES]
            image = jnp.sum(
                products * jnp.concatenate(strict_factors, axis=0), axis=0, keepdims=True
            )
            for target in range(ROWS):
                lanes = slice(target * WIDTH * 16, (target + 1) * WIDTH * 16)
                zex[target, a : a + 1, 0 : WIDTH * 16] = 2.0 * image[:, lanes]
        for t in range(LINES):
            pvec[t] = sums[t * 8 : t * 8 + 8]

    @pl.when(step == 0)
    def _():
        @pl.when(col < HALF)
        def _():
            prepare_panel()
            prepare_columns()

        @pl.when(col >= HALF)
        def _():
            exchange()

    @pl.when(col < HALF)
    def _():
        lax.fori_loop(0, Q_STEP, one_block, 0)

        @pl.when(step == pl.num_programs(0) - 1)
        def _():
            finish()


def pair_products(blocks, panel, masks, cols, ctrial, ptrial, density, rvec, trial, window):
    shapes = [
        jax.ShapeDtypeStruct((ROWS, 8, 128), F32),
        jax.ShapeDtypeStruct((SLOTS, 8, 128), F32),
        jax.ShapeDtypeStruct((LINES, 8, 256), F32),
        jax.ShapeDtypeStruct((ROWS, 8, 128), F32),
    ]

    def whole(array):
        zeros = (0,) * len(array.shape)
        return pl.BlockSpec(array.shape, lambda i: zeros)

    operands = (panel, masks, cols, ctrial, ptrial, density, rvec, trial, window)
    return pl.pallas_call(
        pair_kernel,
        name="pairs",
        grid=(SIDE // Q_STEP,),
        out_shape=shapes,
        in_specs=[pl.BlockSpec((LINES, Q_STEP, 256, 256), lambda i: (0, i, 0, 0))]
        + [whole(x) for x in operands],
        out_specs=[whole(x) for x in shapes],
        scratch_shapes=[
            pltpu.VMEM((2, LINES * 8 * SIDE, 128), F32),
            pltpu.VMEM((2, LINES * 4 * RING, 128), F32),
            pltpu.VMEM((2, LINES * 4 * RING, 128), F32),
            pltpu.VMEM((LINES * LINES * RING, 128), F32),
            pltpu.VMEM((2, LINES * 4 * RING, 128), F32),
            pltpu.VMEM((2, SLOTS * 64, 128), F32),
            pltpu.VMEM((SLOTS * 32, 256), BF16),
            pltpu.VMEM((2, SLOTS * 32, 128), F32),
            pltpu.VMEM((2, SLOTS * 32, 128), F32),
        ],
        compiler_params=pltpu.CompilerParams(vmem_limit_bytes=48 * 1024 * 1024),
    )(blocks, *operands)


def reduce_kernel(
    zrow,
    zcol,
    pvec,
    zex,
    density,
    coulomb,
    row_image,
    col_image,
    rbuf,
    cbuf,
    dbuf,
    pbuf,
    ebuf,
    fbuf,
    ssum,
    dens_v,
    send,
    recv,
    local,
):
    row, col = lax.axis_index("row"), lax.axis_index("col")
    first = row * WIDTH
    greet()

    def to(source, target, number, arrives, device):
        return remote(source, target, send.at[number], recv.at[arrives], device)

    def row_peers():
        return [(step, lax.rem(row + step, ROWS)) for step in range(1, ROWS)]

    def row_sources():
        return [(step, lax.rem(row + ROWS - step, ROWS)) for step in range(1, ROWS)]

    def final_copies():
        copies = []
        for step in range(1, 2 * HALF):
            peer = lax.rem(col + step, 2 * HALF)
            copies.append(to(ssum, fbuf.at[col], 8 + step, 16 + col, (row, peer)))
        return copies

    @pl.when(col < HALF)
    def _():
        copies = [
            to(zrow.at[peer], rbuf.at[row], step, step, (peer, col)) for step, peer in row_peers()
        ]
        near = to(zcol.at[0:LINES], cbuf, 0, 8, (row, col + HALF))
        for copy in copies:
            copy.start()
        near.start()

        @pl.when(col < HALF - 1)
        def _():
            far = to(zcol.at[LINES:SLOTS], dbuf, 8, 9, (row, col + HALF + 1))
            far.start()
            far.wait_send()

        total = zrow[row]
        for step, source in row_sources():
            to(zrow.at[0], rbuf.at[source], 0, step, (source, col)).wait_recv()
            total += rbuf[source]
        ssum[...] = total
        for copy in copies:
            copy.wait_send()
        near.wait_send()

    @pl.when(col >= HALF)
    def _():
        copies = [
            to(zex.at[peer], ebuf.at[row], step, step, (peer, col)) for step, peer in row_peers()
        ]
        for copy in copies:
            copy.start()

        @pl.when(col > HALF)
        def _():
            part = to(pvec, pbuf.at[col - HALF], 0, 24 + col, (row, HALF))
            part.start()
            part.wait_send()

        @pl.when(col == HALF)
        def _():
            fetch = pltpu.make_async_copy(density.at[:, pl.ds(first, WIDTH)], dens_v, local.at[0])
            fetch.start()
            sums = [pvec[t] for t in range(LINES)]
            for j in range(1, HALF):
                to(pvec, pbuf.at[j], 0, 24 + HALF + j, (row, HALF)).wait_recv()
                for t in range(LINES):
                    sums[t] += pbuf[j, t]
            fetch.wait()
            total = jnp.zeros((8, 128), F32)
            lanes = WIDTH * 16
            own = iota((8, lanes), 1) // 16 == iota((8, lanes), 0)
            for t in range(LINES):
                scaled = (dens_v[t].astype(F32) * coulomb[...]).astype(BF16)
                scaled = scaled.reshape(lanes, 256)
                high = sums[t].astype(BF16)
                low = (sums[t] - high.astype(F32)).astype(BF16)
                products = dot(jnp.concatenate([high, low], axis=0), scaled, (1, 1))
                products = jnp.where(own, products[0:8] + products[8:16], 0.0)
                fold = ones_where(
                    iota((lanes, 128), 0) % 16 + t * 16 == iota((lanes, 128), 1), F32
                )
                total += dot(products, fold, precision=HIGHEST)
            ssum[...] = 2.0 * total

        for copy in copies:
            copy.wait_send()

    @pl.when(col <= HALF)
    def _():
        for copy in final_copies():
            copy.start()
        fbuf[col] = ssum[...]

    for source in range(HALF + 1):

        @pl.when(col != source)
        def _():
            to(ssum, fbuf.at[source], 0, 16 + source, (row, source)).wait_recv()

    total = fbuf[0]
    for source in range(1, HALF + 1):
        total += fbuf[source]
    choose = ones_where(iota((8, 128), 1) == iota((8, 128), 0) * 16 + col, F32)
    picked = dot(choose, total, (1, 1), HIGHEST)
    row_image[0] = picked[0:LINES, 0:WIDTH]

    @pl.when(col <= HALF)
    def _():
        for copy in final_copies():
            copy.wait_send()

    @pl.when(col < HALF)
    def _():
        col_image[...] = jnp.zeros_like(col_image)

    @pl.when(col >= HALF)
    def _():
        exchange = zex[row]
        for step, source in row_sources():
            to(zex.at[0], ebuf.at[source], 0, step, (source, col)).wait_recv()
            exchange += ebuf[source]
        to(zcol.at[0:LINES], cbuf, 0, 8, (row, HALF)).wait_recv()

        @pl.when(col > HALF)
        def _():
            to(zcol.at[LINES:SLOTS], dbuf, 0, 9, (row, HALF)).wait_recv()

        picks = ones_where(iota((16, 128), 0) == iota((16, 128), 1), F32)
        folds = iota((16, 128), 1) % 16 == iota((16, 128), 0)
        spots = ones_where(iota((8, 128), 1) // 16 == iota((8, 128), 0), F32)
        for a in range(LINES):
            direct = cbuf[a]
            if a < LINES - 1:
                direct += jnp.where(col > HALF, dbuf[a], 0.0)
            image = dot(picks, direct, (1, 1), HIGHEST)
            values = jnp.where(folds, exchange[a : a + 1], 0.0)
            image += dot(values, spots, (1, 1), HIGHEST)
            col_image[:, a, :] = image[:, 0:WIDTH]


def reduce_parts(zrow, zcol, pvec, zex, density, coulomb):
    return pl.pallas_call(
        reduce_kernel,
        name="reduce",
        out_shape=[
            jax.ShapeDtypeStruct((1, LINES, WIDTH), F32),
            jax.ShapeDtypeStruct((16, LINES, WIDTH), F32),
        ],
        in_specs=[VMEM, VMEM, VMEM, VMEM, ANY, VMEM],
        out_specs=[VMEM, VMEM],
        scratch_shapes=[
            pltpu.VMEM((ROWS, 8, 128), F32),
            pltpu.VMEM((LINES, 8, 128), F32),
            pltpu.VMEM((SLOTS - LINES, 8, 128), F32),
            pltpu.VMEM((HALF, LINES, 8, 256), F32),
            pltpu.VMEM((ROWS, 8, 128), F32),
            pltpu.VMEM((HALF + 1, 8, 128), F32),
            pltpu.VMEM((8, 128), F32),
            pltpu.VMEM((LINES, WIDTH, 16, 256), BF16),
            pltpu.SemaphoreType.DMA((24,)),
            pltpu.SemaphoreType.DMA((40,)),
            pltpu.SemaphoreType.DMA((1,)),
        ],
        compiler_params=pltpu.CompilerParams(collective_id=1, has_side_effects=True),
    )(zrow, zcol, pvec, zex, density, coulomb)


def local(band_factors, pair_density, screened, coulomb, window_mask, trial_vector):
    trial = trial_vector.transpose(1, 2, 0)
    scale = coulomb.reshape(1, 256)
    panel, masks, cols, ctrial, ptrial, rvec = gather(
        band_factors, pair_density, trial, window_mask, scale
    )
    parts = pair_products(
        screened, panel, masks, cols, ctrial, ptrial, pair_density, rvec, trial, window_mask
    )
    row_image, col_image = reduce_parts(*parts, pair_density, scale)
    return row_image, col_image


def solution(mesh):
    placed = (
        P("col", None, None, None),
        P("col", None, None, None),
        P("col", None, None, None),
        P(),
        P(None, "row", None),
        P(None, "col", None),
    )
    return jax.shard_map(
        local,
        mesh=mesh,
        in_specs=placed,
        out_specs=(P("col", None, "row"), P(None, "col", "row")),
        check_vma=False,
    )
```

time: 813 us -> 78.7 us (0.10); the launches traced: 798 us -> 77.7 us
  blocking collectives: 415 us -> 0 us
  local copies, waits for them, and re-layouts: 153 us -> 14.5 us
  matrix products: 136 us -> 0 us
  Pallas kernels: 0 us -> 62.6 us
  waiting for transfers between devices: 37.4 us -> 0 us
  starting transfers between devices: 26.8 us -> 0 us
  between operations: 15.8 us -> 0.68 us
  other arithmetic: 14 us -> 0 us
    psum x1 -> x0, blocking collectives: 328 us -> none  [broadcast(): return lax.psum(block, axis)]
    dot_general x14 -> x0, matrix products: 136 us -> none  [the longest x3 79.3 us: slab_terms(): jnp.einsum('tqiach,tqivwh->tqivawc', mixed_pair, right_pair, preferred_el...]
    unnamed x2 -> x0, blocking collectives: 87.7 us -> none
    pallas_call x0 -> x3, Pallas kernels: none -> 62.6 us  [the longest x1 26 us: gather(): pl.pallas_call(gather_kernel, name='gather', out_shape=shapes, in_specs=[...]
    psum x1 -> x0, waiting for transfers between devices: 37.4 us -> none  [broadcast(): return lax.psum(block, axis)]
    transpose x3 -> x0, local copies, waits for them, and re-layouts: 37 us -> none  [slab_terms(): jnp.einsum('tqiach,tqivwh->tqivawc', mixed_pair, right_pair, preferred_el...]
    gather x18 -> x0, local copies, waits for them, and re-layouts: 32.1 us -> none  [the longest x3 19.4 us: slab_terms(): chosen_pairs = jnp.take(col_pairs, places, axis=1)]
    mul x14 -> x0, local copies, waits for them, and re-layouts: 27.5 us -> none  [the longest x12 24.9 us: slab_terms(): row_bands[:, None, :, :band_half, None, :]]
  transfers between devices with their start and end apart: 7 -> 0, of which waited for: 1 -> 0; matrix products, arithmetic and copies ran while one was open for 21% -> 0% of each run, Pallas kernels for 0% -> 0%
where the time goes in v1:
time: 78.7 us; the launch traced here: 77.7 us
  Pallas kernels  62.6 us (80%)
  local copies, waits for them, and re-layouts  14.5 us (18%)
    pallas_call x1, Pallas kernels, gather(): pl.pallas_call(gather_kernel, name='gather', out_shape=shapes, in_specs=[...  26 us
    pallas_call x1, Pallas kernels, pair_products(): pl.pallas_call(pair_kernel, name='pairs', grid=(SIDE // Q_STEP,), out_sha...  20.7 us
    pallas_call x1, Pallas kernels, reduce_parts(): pl.pallas_call(reduce_kernel, name='reduce', out_shape=[jax.ShapeDtypeStr...  15.9 us
    unnamed x27, local copies, waits for them, and re-layouts  11.8 us
    pallas_call x2, local copies, waits for them, and re-layouts, reduce_parts(): pl.pallas_call(reduce_kernel, name='reduce', out_shape=[jax.ShapeDtypeStr...  2.69 us

profile of v1, /device:TPU:1, one launch (start us, length us, event | category | flops | bytes accessed | tf_op | source)
XLA Modules:
  0.0 77.7 jit_solution(3196964690592160021)
XLA Ops:
  0.6 1.4 %copy.8 = bf16[16,3,48]{0,2,1:T(8,128)(2,1)} copy(bf16[16,3,48]{2,0,1:T(8,128)(2,1)} %param.11) | data formatting | bytes 9216 | tf_op args[5]
  2.0 26.0 %gather.1 = (bf16[8,3,6,8,256]{4,3,2,1,0:T(8,128)(2,1)}, s32[8,3,6,48]{3,2,1,0:T(8,128)}, bf16[5,6,8,256]{3,2,1,0:T(8,128)(2,1)}, bf16[2,3,48,16]{3,2,1,0:T(8,12...) custom-call(bf16[3,48,8,256]{3,2,1,0:T(8,128)(2,1)} %bands.1, bf16[3,48,16,256]{3,2,1,0:T(8,128)(2,1)} %density.5, ...), custom_call_target="tpu_custom_call" | custom-call | tf_op jit(solution)/shard_map/gather/pallas_call | solution.py:217
  28.0 0.0 copy-start
  28.0 1.3 %copy-done = bf16[3,48,16,256]{3,2,1,0:T(8,128)(2,1)S(1)} copy-done((bf16[3,48,16,256]{3,2,1,0:T(8,128)(2,1)S(1)}, bf16[3,48,16,256]{3,2,1,0:T(8,128)(2,1)}, u32[]{:S(2)}) %copy-start) | copy-done | bytes 1179672
  29.3 0.0 copy-start.1
  29.3 1.1 %copy-done.1 = bf16[8,3,6,8,256]{4,3,2,1,0:T(8,128)(2,1)S(1)} copy-done((bf16[8,3,6,8,256]{4,3,2,1,0:T(8,128)(2,1)S(1)}, bf16[8,3,6,8,256]{4,3,2,1,0:T(8,128)(2,1)}, u32[]{:S(2)}) %copy-start.1) | copy-done | bytes 589848
  30.4 0.0 copy-start.2
  30.4 0.8 copy-done.2
  31.1 0.0 copy-start.3
  31.1 0.9 %copy-done.3 = bf16[5,6,8,256]{3,2,1,0:T(8,128)(2,1)S(1)} copy-done((bf16[5,6,8,256]{3,2,1,0:T(8,128)(2,1)S(1)}, bf16[5,6,8,256]{3,2,1,0:T(8,128)(2,1)}, u32[]{:S(2)}) %copy-start.3) | copy-done | bytes 122904
  32.0 0.9 %copy-done.4 = s32[8,3,6,48]{3,2,1,0:T(8,128)S(1)} copy-done((s32[8,3,6,48]{3,2,1,0:T(8,128)S(1)}, s32[8,3,6,48]{3,2,1,0:T(8,128)}, u32[]{:S(2)}) %copy-start.4) | copy-done | bytes 27672
  32.9 0.9 %copy-done.5 = bf16[2,3,48,16]{3,2,1,0:T(8,128)(2,1)S(1)} copy-done((bf16[2,3,48,16]{3,2,1,0:T(8,128)(2,1)S(1)}, bf16[2,3,48,16]{3,2,1,0:T(8,128)(2,1)}, u32[]{:S(2)}) %copy-start.5) | copy-done | bytes 9240
  33.8 0.7 copy-done.6
  34.5 0.8 copy-done.7
  35.3 0.7 copy-done.11
  36.0 20.7 %pairs.1 = (f32[8,8,128]{2,1,0:T(8,128)S(1)}, f32[5,8,128]{2,1,0:T(8,128)S(1)}, f32[3,8,256]{2,1,0:T(8,128)S(1)}, f32[8,8,128]{2,1,0:T(8,128)S(1)}) custom-call(bf16[3,48,256,256]{3,2,1,0:T(8,128)(2,1)} %blocks.1, bf16[8,3,6,8,256]{4,3,2,1,0:T(8,128)(2,1)S(1)} %copy-done.1, s32[8,3,6,48]{3,2,1,0:T(8,128)S(1)} %copy-done.4, ...), custom_call_target="tpu_custom_call" | custom-call | tf_op jit(solution)/shard_map/pairs/pallas_call | solution.py:498
  56.7 0.0 copy-start.8
  56.7 0.6 copy-done.8
  57.3 0.6 copy-done.9
  57.9 0.6 copy-done.10
  58.5 0.6 copy-done.12
  59.1 15.9 %reduce.1 = (f32[1,3,6]{2,1,0:T(4,128)}, f32[16,3,6]{2,1,0:T(4,128)}) custom-call(f32[8,8,128]{2,1,0:T(8,128)} %copy-done.8, f32[5,8,128]{2,1,0:T(8,128)} %copy-done.12, f32[3,8,256]{2,1,0:T(8,128)} %copy-done.10, f32[8,8,128]{2,1,0:T(8,128)} %copy-done.9, bf16[3,48,16,256]{3,2,1,0:T(8,128)(2,1)} %density.5, f32[1,256]{1,0:T(1,128)} %bitcast.6), custom_call_target="tpu_custom_call" | custom-call | tf_op jit(solution)/shard_map/reduce/pallas_call | solution.py:684
  75.0 1.2 %copy.9 = f32[1,3,6]{2,0,1:T(1,128)} copy(f32[1,3,6]{2,1,0:T(4,128)} %get-tuple-element.22) | data formatting | bytes 144 | tf_op jit(solution)/shard_map/reduce/pallas_call | solution.py:684
  76.3 1.4 %copy.10 = f32[16,3,6]{0,2,1:T(8,128)} copy(f32[16,3,6]{2,1,0:T(4,128)} %get-tuple-element.23) | data formatting | bytes 2304 | tf_op jit(solution)/shard_map/reduce/pallas_call | solution.py:684
  (8 shorter events, 0.0 us)
Async XLA Ops:
  28.0 1.3 %copy-start = (bf16[3,48,16,256]{3,2,1,0:T(8,128)(2,1)S(1)}, bf16[3,48,16,256]{3,2,1,0:T(8,128)(2,1)}, u32[]{:S(2)}) copy-start(bf16[3,48,16,256]{3,2,1,0:T(8,128)(2,1)} %density.5) | copy-start | bytes 3538948
  29.3 1.1 %copy-start.1 = (bf16[8,3,6,8,256]{4,3,2,1,0:T(8,128)(2,1)S(1)}, bf16[8,3,6,8,256]{4,3,2,1,0:T(8,128)(2,1)}, u32[]{:S(2)}) copy-start(bf16[8,3,6,8,256]{4,3,2,1,0:T(8,128)(2,1)} %get-tuple-element.12.panel) | copy-start | bytes 1769476
  30.4 0.8 copy-start.2
  31.1 0.9 %copy-start.3 = (bf16[5,6,8,256]{3,2,1,0:T(8,128)(2,1)S(1)}, bf16[5,6,8,256]{3,2,1,0:T(8,128)(2,1)}, u32[]{:S(2)}) copy-start(bf16[5,6,8,256]{3,2,1,0:T(8,128)(2,1)} %get-tuple-element.14.cols) | copy-start | bytes 368644
  32.0 0.9 %copy-start.4 = (s32[8,3,6,48]{3,2,1,0:T(8,128)S(1)}, s32[8,3,6,48]{3,2,1,0:T(8,128)}, u32[]{:S(2)}) copy-start(s32[8,3,6,48]{3,2,1,0:T(8,128)} %get-tuple-element.13.masks) | copy-start | bytes 82948
  32.9 0.9 %copy-start.5 = (bf16[2,3,48,16]{3,2,1,0:T(8,128)(2,1)S(1)}, bf16[2,3,48,16]{3,2,1,0:T(8,128)(2,1)}, u32[]{:S(2)}) copy-start(bf16[2,3,48,16]{3,2,1,0:T(8,128)(2,1)} %get-tuple-element.15.ctrial) | copy-start | bytes 27652
  33.8 0.7 copy-start.6
  34.5 0.8 copy-start.7
  35.3 0.7 copy-start.11
  56.7 0.6 copy-start.8
  57.3 0.6 copy-start.9
  57.9 0.6 copy-start.10
  58.5 0.6 copy-start.12

commit v2 on v1

v2 whole, which is shorter than its diff:
```python
import functools

import jax
import jax.numpy as jnp
from jax import lax
from jax.experimental import pallas as pl
from jax.experimental.pallas import tpu as pltpu
from jax.sharding import PartitionSpec as P

MESH = pl.DeviceIdType.MESH
F32 = jnp.float32
BF16 = jnp.bfloat16
SIDE = 48
ROWS = 8
WIDTH = 6
LINES = 3
HALF = 8
SLOTS = 2 * LINES - 1
RING = SIDE + 8
Q_STEP = 4
HIGHEST = lax.Precision.HIGHEST
ANY = pl.BlockSpec(memory_space=pl.ANY)
VMEM = pl.BlockSpec(memory_space=pltpu.VMEM)


def iota(shape, axis):
    return lax.broadcasted_iota(jnp.int32, shape, axis)


def dot(a, b, contract=(1, 0), precision=None):
    return lax.dot_general(
        a,
        b,
        (((contract[0],), (contract[1],)), ((), ())),
        preferred_element_type=F32,
        precision=precision,
    )


def ones_where(condition, dtype=BF16):
    return jnp.where(condition, 1.0, 0.0).astype(dtype)


def pick_rows(trial_line, first):
    pick = ones_where(iota((8, SIDE), 1) == first + iota((8, SIDE), 0))
    return dot(pick, trial_line, (1, 1)).astype(BF16)


def block_diagonal(trial_line, first, copies):
    rows = pick_rows(trial_line, first)
    tiled = dot(rows, ones_where(iota((16, copies * 16), 1) % 16 == iota((16, copies * 16), 0)))
    return jnp.where(iota(tiled.shape, 1) // 16 == iota(tiled.shape, 0), tiled, 0.0)


def greet():
    row, col = lax.axis_index("row"), lax.axis_index("col")
    barrier = pltpu.get_barrier_semaphore()
    for step in range(1, ROWS):
        pl.semaphore_signal(
            barrier, inc=1, device_id=(lax.rem(row + step, ROWS), col), device_id_type=MESH
        )
    for step in range(1, 2 * HALF):
        pl.semaphore_signal(
            barrier, inc=1, device_id=(row, lax.rem(col + step, 2 * HALF)), device_id_type=MESH
        )
    pl.semaphore_wait(barrier, ROWS + 2 * HALF - 2)


def remote(source, target, send_sem, recv_sem, device):
    return pltpu.make_async_remote_copy(
        src_ref=source,
        dst_ref=target,
        send_sem=send_sem,
        recv_sem=recv_sem,
        device_id=device,
        device_id_type=MESH,
    )


def panel_product_kernel(
    bands,
    density,
    blocks,
    trial,
    window,
    trial_v,
    coulomb,
    row_image,
    col_image,
    w_buf,
    dens,
    pieces,
    cols,
    ctrial,
    ptrial,
    rsend,
    rvec,
    flat,
    left_t,
    y_row,
    keep_t,
    r_sum,
    col_flat,
    u_col,
    y_col,
    c_sum,
    zrow,
    zcol,
    pvec,
    zex,
    rbuf,
    cbuf,
    dbuf,
    pbuf,
    ebuf,
    fbuf,
    ssum,
    send,
    recv,
    local,
    w_sem,
):
    row, col = lax.axis_index("row"), lax.axis_index("col")
    first = row * WIDTH
    core = lax.rem(col, 2)
    twin = (row, col + 1 - 2 * core)
    halves = (slice(0, 128), slice(128, 256))
    spread = ones_where(iota((16, 2048), 1) // 128 == iota((16, 2048), 0))

    def to(source, target, number, arrives, device):
        return remote(source, target, send.at[number], recv.at[arrives], device)

    def row_peers():
        return [(step, lax.rem(row + step, ROWS)) for step in range(1, ROWS)]

    def row_sources():
        return [(step, lax.rem(row + ROWS - step, ROWS)) for step in range(1, ROWS)]

    COLS, NEXT, CT, CTN, PT, OWN, RVEC = 0, 1, 2, 3, 4, 5, 6
    PIECE, TWIN, RSUM, CSUM, DSUM, FINAL, PVEC = 8, 16, 24, 32, 33, 34, 44
    S_PIECE, S_TWIN, S_RSUM, S_CSUM, S_DSUM, S_FINAL, S_SWAP = 0, 8, 16, 24, 25, 32, 48

    def lane(expanded, s):
        return expanded[:, s * 128 : (s + 1) * 128]

    def chunk(number):
        return pltpu.make_async_copy(
            blocks.at[:, pl.ds(number * Q_STEP, Q_STEP)],
            w_buf.at[:, pl.ds(number * Q_STEP, Q_STEP)],
            w_sem.at[number],
        )

    def fetch_density():
        return pltpu.make_async_copy(density, dens, local.at[0])

    def store_ring(table, h, number, value):
        base = number * RING
        table[h, base : base + SIDE, :] = value
        table[h, base + SIDE : base + RING, :] = value[0:8]

    def unpack_piece(half, source):
        for t in range(LINES):
            value = pieces[half, source, t].astype(F32).reshape(WIDTH * 4, 256)
            base = pl.multiple_of((t * SIDE + source * WIDTH + half * (WIDTH // 2)) * 8, 8)
            for h in range(2):
                flat[h, pl.ds(base, WIDTH * 4), :] = value[:, halves[h]]

    def prepare_panel():
        for t in range(LINES):
            line = jnp.transpose(ptrial[t].astype(F32)).astype(BF16)
            expanded = dot(line, spread)
            for h in range(2):

                def band(number):
                    return flat[h, pl.ds(t * 8 * SIDE + number, SIDE, stride=8), :]

                for c in range(4):
                    store_ring(left_t, h, t * 4 + c, band(c))
                valence = [band(4 + v) for v in range(4)]
                for c in range(4):
                    total = valence[0] * lane(expanded, c)
                    for v in range(1, 4):
                        total += valence[v] * lane(expanded, 4 * v + c)
                    store_ring(y_row, h, t * 4 + c, total)
        places = iota((8, 256), 1)
        rows = iota((8, 256), 0)
        for e in range(LINES):
            line = HALF * LINES + col * LINES + e + rows
            for source in range(ROWS):
                for half in range(2):
                    for i in range(WIDTH // 2):
                        held = pieces[half, source, LINES, i].astype(F32)
                        held = jnp.where((places == line) & (rows < LINES), held, 0.0)
                        factor = jnp.sum(held, axis=1, keepdims=True)
                        factor = jnp.broadcast_to(factor, (8, 128))
                        b = source * WIDTH + half * (WIDTH // 2) + i
                        for t in range(LINES):
                            base = (e * LINES + t) * RING
                            keep_t[base + b : base + b + 1, :] = factor[t : t + 1]
                            if b < 8:
                                base += SIDE
                                keep_t[base + b : base + b + 1, :] = factor[t : t + 1]
        r_sum[...] = jnp.zeros_like(r_sum)

    def prepare_columns():
        for a in range(SLOTS):
            value = cols[a].astype(F32).reshape(WIDTH * 8, 256)
            if a >= LINES:
                value = jnp.where(col < HALF - 1, value, 0.0)
            for h in range(2):
                col_flat[h, a * 64 : a * 64 + WIDTH * 8, :] = value[:, halves[h]]
                col_flat[h, a * 64 + WIDTH * 8 : a * 64 + 64, :] = jnp.zeros((16, 128), F32)
        for a in range(SLOTS):
            line = ctrial[a // LINES, a % LINES]
            expanded = dot(pick_rows(line, first), spread)
            if a >= LINES:
                expanded = jnp.where(col < HALF - 1, expanded, 0.0)
            for h in range(2):

                def band(number):
                    return col_flat[h, pl.ds(a * 64 + number, 8, stride=8), :]

                for pair in range(2):
                    both = jnp.concatenate([band(2 * pair), band(2 * pair + 1)], axis=0)
                    u_col[a * 32 + pair * 16 : a * 32 + pair * 16 + 16, halves[h]] = both.astype(
                        BF16
                    )
                valence = [band(4 + v) for v in range(4)]
                for c in range(4):
                    total = valence[0] * lane(expanded, c)
                    for v in range(1, 4):
                        total += valence[v] * lane(expanded, 4 * v + c)
                    y_col[h, (a * 4 + c) * 8 : (a * 4 + c) * 8 + 8, :] = total
        c_sum[...] = jnp.zeros_like(c_sum)

    def one_block(q_value, carry):
        start = lax.rem(first + SIDE - q_value, SIDE)
        inside = (first + iota((8, 128), 0) >= q_value) | (col > 0)
        same = (q_value == 0) & (col == 0)
        for t in range(LINES):

            def rows(table, c, h):
                return table[h, pl.ds((t * 4 + c) * RING + start, 8), :]

            lefts = [[rows(left_t, c, h) for h in range(2)] for c in range(4)]
            backs = [[rows(y_row, c, h) for h in range(2)] for c in range(4)]
            totals = [[None, None] for _ in range(4)]
            for e in range(LINES):
                a = t + e
                factor = keep_t[pl.ds((e * LINES + t) * RING + start, 8), :]
                if e == 0:
                    factor = jnp.where(inside, factor, 0.0)
                tiles = []
                for c in range(4):
                    both = []
                    for h in range(2):
                        kept = lefts[c][h] * factor
                        both.append(jnp.concatenate([kept, kept], axis=0).astype(BF16))
                    both = jnp.concatenate(both, axis=1)
                    for pair in range(2):
                        base = a * 32 + pair * 16
                        tiles.append(both * u_col[base : base + 16, :])
                mixed = dot(jnp.concatenate(tiles, axis=0), w_buf[e, q_value])
                for h in range(2):
                    images = [None] * 4
                    for c in range(4):
                        for d in range(4):
                            base = (c * 4 + d) * 8
                            piece = mixed[base : base + 8, halves[h]]
                            base = (a * 4 + d) * 8
                            part = piece * y_col[h, base : base + 8, :]
                            totals[c][h] = part if totals[c][h] is None else totals[c][h] + part
                            part = piece * backs[c][h]
                            images[d] = part if images[d] is None else images[d] + part
                    for d in range(4):
                        base = (a * 4 + d) * 8
                        image = jnp.where(same, 0.0, images[d]) if e == 0 else images[d]
                        c_sum[h, base : base + 8, :] += image
            for c in range(4):
                for h in range(2):
                    r_sum[h, pl.ds((t * 4 + c) * RING + start, 8), :] += totals[c][h]
        return carry

    def finish():
        lanes = iota((SIDE, 128), 1)
        image = jnp.zeros((SIDE, 128), F32)
        for t in range(LINES):
            for c in range(4):
                base = (t * 4 + c) * RING
                total = []
                for h in range(2):
                    head = r_sum[h, base : base + 8, :] + r_sum[h, base + SIDE : base + RING, :]
                    total.append(
                        jnp.concatenate([head, r_sum[h, base + 8 : base + SIDE, :]], axis=0)
                    )
                for v in range(4):
                    product = 0.0
                    for h in range(2):
                        strided = pl.ds(t * 8 * SIDE + 4 + v, SIDE, stride=8)
                        product += flat[h, strided, :] * total[h]
                    value = jnp.sum(product, axis=1, keepdims=True)
                    image = jnp.where(lanes == t * 16 + 4 * v + c, value, image)
        for target in range(ROWS):
            zrow[target, 0:WIDTH, :] = -image[target * WIDTH : (target + 1) * WIDTH]
            zrow[target, WIDTH:8, :] = jnp.zeros((8 - WIDTH, 128), F32)
        lanes = iota((8, 128), 1)
        for a in range(SLOTS):
            image = jnp.zeros((8, 128), F32)
            for v in range(4):
                for c in range(4):
                    product = 0.0
                    for h in range(2):
                        base = (a * 4 + c) * 8
                        strided = pl.ds(a * 64 + 4 + v, 8, stride=8)
                        product += col_flat[h, strided, :] * c_sum[h, base : base + 8, :]
                    value = jnp.sum(product, axis=1, keepdims=True)
                    image = jnp.where(lanes == 4 * v + c, value, image)
            zcol[a] = -image

    def exchange():
        tile = ones_where(iota((16, SIDE * 16), 1) % 16 == iota((16, SIDE * 16), 0))
        own_point = iota((SIDE, SIDE * 16), 1) // 16 == iota((SIDE, SIDE * 16), 0)
        ones = jnp.ones((8, SIDE), BF16)
        points = iota((8, SIDE * 16), 1) // 16
        row_points = first + iota((8, SIDE * 16), 0)
        places = iota((WIDTH, SIDE), 1)
        wide = jnp.concatenate([rvec[t] for t in range(LINES)], axis=0)
        high = wide.astype(BF16)
        low = (wide - high.astype(F32)).astype(BF16)
        split = jnp.concatenate([high, low], axis=0)
        zex[...] = jnp.zeros_like(zex)
        sums = jnp.zeros((8 * LINES, 256), F32)
        for a in range(LINES):
            line = col * LINES + a
            transposed = jnp.transpose(trial_v[a].astype(F32)).astype(BF16)
            values = jnp.where(own_point, dot(transposed, tile), 0.0).astype(BF16)
            values = dot(ones, values)
            kept_values = []
            strict_factors = []
            for t in range(LINES):
                row_line = HALF * LINES + t
                held = jnp.where(places == line, window[t], 0).astype(F32)
                held = jnp.sum(held, axis=1, keepdims=True)
                held = jnp.concatenate([held, jnp.zeros((8 - WIDTH, 1), F32)], axis=0)
                kept = (line > row_line) | ((line == row_line) & (points >= row_points))
                strict = (line > row_line) | ((line == row_line) & (points > row_points))
                kept_values.append(jnp.where(kept, held, 0.0) * values)
                strict_factors.append(jnp.where(strict, held, 0.0))
            table = dens[a].reshape(SIDE * 16, 256)
            sums += dot(jnp.concatenate(kept_values, axis=0).astype(BF16), table)
            products = dot(split, table, (1, 1))
            products = products[0 : 8 * LINES] + products[8 * LINES : 16 * LINES]
            image = jnp.sum(
                products * jnp.concatenate(strict_factors, axis=0), axis=0, keepdims=True
            )
            for target in range(ROWS):
                lanes = slice(target * WIDTH * 16, (target + 1) * WIDTH * 16)
                zex[target, a : a + 1, 0 : WIDTH * 16] = 2.0 * image[:, lanes]
        for t in range(LINES):
            pvec[t] = sums[t * 8 : t * 8 + 8]

    def row_vectors():
        for t in range(LINES):
            diagonal = block_diagonal(trial_v[t], first, WIDTH).astype(BF16)
            scaled = (dens[t, pl.ds(first, WIDTH)].astype(F32) * coulomb[...]).astype(BF16)
            rsend[t] = dot(diagonal, scaled.reshape(WIDTH * 16, 256))

    def exchange_rows():
        total = jnp.zeros((8, 128), F32)
        lanes = WIDTH * 16
        own = iota((8, lanes), 1) // 16 == iota((8, lanes), 0)
        for t in range(LINES):
            summed = pvec[t]
            for j in range(1, HALF):
                summed += pbuf[j, t]
            scaled = (dens[t, pl.ds(first, WIDTH)].astype(F32) * coulomb[...]).astype(BF16)
            scaled = scaled.reshape(lanes, 256)
            high = summed.astype(BF16)
            low = (summed - high.astype(F32)).astype(BF16)
            products = dot(jnp.concatenate([high, low], axis=0), scaled, (1, 1))
            products = jnp.where(own, products[0:8] + products[8:16], 0.0)
            fold = ones_where(iota((lanes, 128), 0) % 16 + t * 16 == iota((lanes, 128), 1), F32)
            total += dot(products, fold, precision=HIGHEST)
        ssum[...] = 2.0 * total

    def final_copies():
        copies = []
        for step in range(1, 2 * HALF):
            peer = lax.rem(col + step, 2 * HALF)
            copies.append(to(ssum, fbuf.at[col], S_FINAL + step, FINAL + col, (row, peer)))
        return copies

    def half_panel(half):
        return bands.at[:, pl.ds(first + half * (WIDTH // 2), WIDTH // 2)]

    def panel_copies():
        return [
            to(half_panel(j % 2), pieces.at[j % 2, row, 0:LINES], j, OWN, (row, j))
            for j in range(HALF)
        ] + [to(trial, ptrial, 8 + j, PT, (row, j)) for j in range(HALF)]

    def column_copies():
        near = (row, lax.rem(col + HALF, 2 * HALF))
        own = bands.at[:, pl.ds(first, WIDTH)]
        return [
            to(own, cols.at[0:LINES], 16, COLS, near),
            to(trial, ctrial.at[0], 17, CT, near),
        ]

    def next_copies():
        far = (row, lax.rem(col + HALF - 1, 2 * HALF))
        own = bands.at[0 : LINES - 1, pl.ds(first, WIDTH)]
        return [
            to(own, cols.at[LINES:SLOTS], 18, NEXT, far),
            to(trial, ctrial.at[1], 19, CTN, far),
        ]

    def vector_copies():
        return [to(rsend, rvec, 20 + j, RVEC, (row, HALF + j)) for j in range(1, HALF)]

    def piece_copies():
        own = pieces.at[core, row]
        return [to(own, own, S_TWIN, TWIN, twin)] + [
            to(own, own, S_PIECE + step, PIECE + step, (peer, col)) for step, peer in row_peers()
        ]

    def twin_copies():
        return [
            to(pieces.at[core, source], pieces.at[core, source], S_TWIN + step, TWIN + step, twin)
            for step, source in row_sources()
        ]

    def sum_copies():
        return [
            to(zrow.at[peer], rbuf.at[row], S_RSUM + step, RSUM + step, (peer, col))
            for step, peer in row_peers()
        ]

    def near_sum():
        return to(zcol.at[0:LINES], cbuf, S_CSUM, CSUM, (row, lax.rem(col + HALF, 2 * HALF)))

    def far_sum():
        return to(
            zcol.at[LINES:SLOTS], dbuf, S_DSUM, DSUM, (row, lax.rem(col + HALF + 1, 2 * HALF))
        )

    def exchange_copies():
        return [
            to(zex.at[peer], ebuf.at[row], S_SWAP + step, RSUM + step, (peer, col))
            for step, peer in row_peers()
        ]

    def part_copy():
        return to(pvec, pbuf.at[col - HALF], 8, PVEC + col - HALF, (row, HALF))

    @pl.when(col < HALF)
    def _():
        for number in range(SIDE // Q_STEP):
            chunk(number).start()
        for i in range(WIDTH // 2):
            held = jnp.where(core == 0, window[:, i], window[:, WIDTH // 2 + i]).astype(F32)
            held = jnp.concatenate([held, jnp.zeros((8 - LINES, SIDE), F32)], axis=0)
            held = jnp.concatenate([held, jnp.zeros((8, 256 - SIDE), F32)], axis=1)
            pieces[core, row, LINES, i] = held.astype(BF16)

    @pl.when(col >= HALF)
    def _():
        fetch_density().start()

    greet()

    @pl.when(col < HALF)
    def _():
        to(half_panel(0), pieces.at[core, row, 0:LINES], 0, OWN, (row, HALF)).wait_recv()
        for copy in piece_copies():
            copy.start()
        to(cols.at[0:LINES], cols.at[0:LINES], 0, COLS, (row, HALF)).wait_recv()
        to(trial, ctrial.at[0], 0, CT, (row, HALF)).wait_recv()

        @pl.when(col < HALF - 1)
        def _():
            to(cols.at[LINES:SLOTS], cols.at[LINES:SLOTS], 0, NEXT, (row, HALF)).wait_recv()
            to(trial, ctrial.at[1], 0, CTN, (row, HALF)).wait_recv()

        prepare_columns()
        unpack_piece(core, row)
        forwards = twin_copies()
        for (step, source), forward in zip(row_sources(), forwards):
            piece = pieces.at[core, source]
            to(piece, piece, 0, PIECE + step, (source, col)).wait_recv()
            forward.start()
            unpack_piece(core, source)
        piece = pieces.at[1 - core, row]
        to(piece, piece, 0, TWIN, twin).wait_recv()
        unpack_piece(1 - core, row)
        for step, source in row_sources():
            piece = pieces.at[1 - core, source]
            to(piece, piece, 0, TWIN + step, twin).wait_recv()
            unpack_piece(1 - core, source)
        to(trial, ptrial, 0, PT, (row, HALF)).wait_recv()
        prepare_panel()

        def one_chunk(number, carry):
            chunk(number).wait()
            return lax.fori_loop(number * Q_STEP, (number + 1) * Q_STEP, one_block, carry)

        lax.fori_loop(0, SIDE // Q_STEP, one_chunk, 0)
        finish()
        for copy in sum_copies():
            copy.start()
        near_sum().start()

        @pl.when(col < HALF - 1)
        def _():
            far_sum().start()

        total = zrow[row]
        for step, source in row_sources():
            to(zrow.at[0], rbuf.at[source], 0, RSUM + step, (source, col)).wait_recv()
            total += rbuf[source]
        ssum[...] = total

    @pl.when(col >= HALF)
    def _():
        @pl.when(col == HALF)
        def _():
            for copy in panel_copies():
                copy.start()

        for copy in column_copies():
            copy.start()

        @pl.when(col > HALF)
        def _():
            for copy in next_copies():
                copy.start()

        fetch_density().wait()

        @pl.when(col == HALF)
        def _():
            row_vectors()
            for copy in vector_copies():
                copy.start()
            rvec[...] = rsend[...]

        @pl.when(col > HALF)
        def _():
            to(rsend, rvec, 0, RVEC, (row, HALF)).wait_recv()

        exchange()
        for copy in exchange_copies():
            copy.start()

        @pl.when(col > HALF)
        def _():
            part_copy().start()

        @pl.when(col == HALF)
        def _():
            for j in range(1, HALF):
                to(pvec, pbuf.at[j], 0, PVEC + j, (row, HALF)).wait_recv()
            exchange_rows()

    @pl.when(col <= HALF)
    def _():
        for copy in final_copies():
            copy.start()
        fbuf[col] = ssum[...]

    @pl.when(col < HALF)
    def _():
        col_image[...] = jnp.zeros_like(col_image)

    @pl.when(col >= HALF)
    def _():
        swapped = zex[row]
        for step, source in row_sources():
            to(zex.at[0], ebuf.at[source], 0, RSUM + step, (source, col)).wait_recv()
            swapped += ebuf[source]
        to(zcol.at[0:LINES], cbuf, 0, CSUM, (row, HALF)).wait_recv()

        @pl.when(col > HALF)
        def _():
            to(zcol.at[LINES:SLOTS], dbuf, 0, DSUM, (row, HALF)).wait_recv()

        picks = ones_where(iota((16, 128), 0) == iota((16, 128), 1), F32)
        folds = iota((16, 128), 1) % 16 == iota((16, 128), 0)
        spots = ones_where(iota((8, 128), 1) // 16 == iota((8, 128), 0), F32)
        for a in range(LINES):
            direct = cbuf[a]
            if a < LINES - 1:
                direct += jnp.where(col > HALF, dbuf[a], 0.0)
            image = dot(picks, direct, (1, 1), HIGHEST)
            values = jnp.where(folds, swapped[a : a + 1], 0.0)
            image += dot(values, spots, (1, 1), HIGHEST)
            col_image[:, a, :] = image[:, 0:WIDTH]

    for source in range(HALF + 1):

        @pl.when(col != source)
        def _():
            to(ssum, fbuf.at[source], 0, FINAL + source, (row, source)).wait_recv()

    total = fbuf[0]
    for source in range(1, HALF + 1):
        total += fbuf[source]
    choose = ones_where(iota((8, 128), 1) == iota((8, 128), 0) * 16 + col, F32)
    picked = dot(choose, total, (1, 1), HIGHEST)
    row_image[0] = picked[0:LINES, 0:WIDTH]

    @pl.when(col < HALF)
    def _():
        for copy in piece_copies() + twin_copies() + sum_copies() + [near_sum()]:
            copy.wait_send()

        @pl.when(col < HALF - 1)
        def _():
            far_sum().wait_send()

    @pl.when(col >= HALF)
    def _():
        for copy in column_copies() + exchange_copies():
            copy.wait_send()

        @pl.when(col > HALF)
        def _():
            for copy in next_copies() + [part_copy()]:
                copy.wait_send()

        @pl.when(col == HALF)
        def _():
            for copy in panel_copies() + vector_copies():
                copy.wait_send()

    @pl.when(col <= HALF)
    def _():
        for copy in final_copies():
            copy.wait_send()


def local(band_factors, pair_density, screened, coulomb, window_mask, trial_vector):
    trial = trial_vector.transpose(1, 0, 2)
    vmem = pltpu.VMEM
    row_image, col_image = pl.pallas_call(
        panel_product_kernel,
        name="panel_product",
        out_shape=[
            jax.ShapeDtypeStruct((1, LINES, WIDTH), F32),
            jax.ShapeDtypeStruct((16, LINES, WIDTH), F32),
        ],
        in_specs=[ANY, ANY, ANY, ANY, VMEM, VMEM, VMEM],
        out_specs=[VMEM, VMEM],
        scratch_shapes=[
            vmem((LINES, SIDE, 256, 256), BF16),
            vmem((LINES, SIDE, 16, 256), BF16),
            vmem((2, ROWS, LINES + 1, WIDTH // 2, 8, 256), BF16),
            vmem((SLOTS, WIDTH, 8, 256), BF16),
            vmem((2, LINES, 16, SIDE), BF16),
            vmem((LINES, 16, SIDE), BF16),
            vmem((LINES, 8, 256), F32),
            vmem((LINES, 8, 256), F32),
            vmem((2, LINES * 8 * SIDE, 128), F32),
            vmem((2, LINES * 4 * RING, 128), F32),
            vmem((2, LINES * 4 * RING, 128), F32),
            vmem((LINES * LINES * RING, 128), F32),
            vmem((2, LINES * 4 * RING, 128), F32),
            vmem((2, SLOTS * 64, 128), F32),
            vmem((SLOTS * 32, 256), BF16),
            vmem((2, SLOTS * 32, 128), F32),
            vmem((2, SLOTS * 32, 128), F32),
            vmem((ROWS, 8, 128), F32),
            vmem((SLOTS, 8, 128), F32),
            vmem((LINES, 8, 256), F32),
            vmem((ROWS, 8, 128), F32),
            vmem((ROWS, 8, 128), F32),
            vmem((LINES, 8, 128), F32),
            vmem((SLOTS - LINES, 8, 128), F32),
            vmem((HALF, LINES, 8, 256), F32),
            vmem((ROWS, 8, 128), F32),
            vmem((HALF + 1, 8, 128), F32),
            vmem((8, 128), F32),
            pltpu.SemaphoreType.DMA((56,)),
            pltpu.SemaphoreType.DMA((52,)),
            pltpu.SemaphoreType.DMA((1,)),
            pltpu.SemaphoreType.DMA((SIDE // Q_STEP,)),
        ],
        compiler_params=pltpu.CompilerParams(
            collective_id=0, has_side_effects=True, vmem_limit_bytes=56 * 1024 * 1024
        ),
    )(
        band_factors,
        pair_density,
        screened,
        trial,
        window_mask,
        trial,
        coulomb.reshape(1, 256),
    )
    return row_image, col_image


def solution(mesh):
    placed = (
        P("col", None, None, None),
        P("col", None, None, None),
        P("col", None, None, None),
        P(),
        P(None, "row", None),
        P(None, "col", None),
    )
    return jax.shard_map(
        local,
        mesh=mesh,
        in_specs=placed,
        out_specs=(P("col", None, "row"), P(None, "col", "row")),
        check_vma=False,
    )
```

time: 78.7 us -> 56 us (0.71)
  local copies, waits for them, and re-layouts: 14.5 us -> 2.67 us
  Pallas kernels: 62.6 us -> 52.4 us
    unnamed x27 -> x0, local copies, waits for them, and re-layouts: 11.8 us -> none
    pallas_call x3 -> x1, Pallas kernels: 62.6 us -> 52.4 us  [local(): pl.pallas_call(panel_product_kernel, name='panel_product', out_shape=[jax...]
where the time goes in v2:
time: 56 us; the launch traced here: 55.8 us
  Pallas kernels  52.4 us (94%)
  local copies, waits for them, and re-layouts  2.67 us (5%)
  between operations  0.64 us (1%)
    pallas_call x1, Pallas kernels, local(): pl.pallas_call(panel_product_kernel, name='panel_product', out_shape=[jax...  52.4 us
    pallas_call x2, local copies, waits for them, and re-layouts, local(): pl.pallas_call(panel_product_kernel, name='panel_product', out_shape=[jax...  2.67 us

profile of v2, /device:TPU:1, one launch (start us, length us, event | category | flops | bytes accessed | tf_op | source)
XLA Modules:
  0.0 55.8 jit_solution(9049473792277575926)
XLA Ops:
  0.6 52.4 %panel_product.1 = (f32[1,3,6]{2,1,0:T(4,128)}, f32[16,3,6]{2,1,0:T(4,128)}) custom-call(bf16[3,48,8,256]{3,2,1,0:T(8,128)(2,1)} %bands.1, bf16[3,48,16,256]{3,2,1,0:T(8,128)(2,1)} %density.1, bf16[3,48,256,256]{3,2,1,0:T(8,128)(2,1)} %blocks.1, bf16[3,16,48]{2,1,0:T(8,128)(2,1)} %bitcast.2, s32[3,6,48]{2,1,0:T(8,128)} %window.1, ...), custom_call_target="tpu_custom_call" | custom-call | tf_op jit(solution)/shard_map/panel_product/pallas_call | solution.py:645
  53.1 1.2 %copy.8 = f32[1,3,6]{2,0,1:T(1,128)} copy(f32[1,3,6]{2,1,0:T(4,128)} %get-tuple-element.2) | data formatting | bytes 144 | tf_op jit(solution)/shard_map/panel_product/pallas_call | solution.py:645
  54.3 1.4 %copy.9 = f32[16,3,6]{0,2,1:T(8,128)} copy(f32[16,3,6]{2,1,0:T(4,128)} %get-tuple-element.3) | data formatting | bytes 2304 | tf_op jit(solution)/shard_map/panel_product/pallas_call | solution.py:645

commit v3 on v2

--- a/solution.py
+++ b/solution.py
@@ -17,6 +17,7 @@
 HALF = 8
 SLOTS = 2 * LINES - 1
 RING = SIDE + 8
+BLOCKS = LINES * WIDTH // 2 + 1
 Q_STEP = 4
 HIGHEST = lax.Precision.HIGHEST
 ANY = pl.BlockSpec(memory_space=pl.ANY)
@@ -85,10 +86,11 @@
     window,
     trial_v,
     coulomb,
-    row_image,
-    col_image,
+    row_part,
+    col_part,
     w_buf,
     dens,
+    stage,
     pieces,
     cols,
     ctrial,
@@ -136,9 +138,10 @@
     def row_sources():
         return [(step, lax.rem(row + ROWS - step, ROWS)) for step in range(1, ROWS)]
 
-    COLS, NEXT, CT, CTN, PT, OWN, RVEC = 0, 1, 2, 3, 4, 5, 6
-    PIECE, TWIN, RSUM, CSUM, DSUM, FINAL, PVEC = 8, 16, 24, 32, 33, 34, 44
-    S_PIECE, S_TWIN, S_RSUM, S_CSUM, S_DSUM, S_FINAL, S_SWAP = 0, 8, 16, 24, 25, 32, 48
+    COLS, NEXT, CT, CTN, PT, OWN, RVEC, TWIN, PIECE = 0, 1, 2, 3, 4, 5, 6, 7, 8
+    RSUM, CSUM, DSUM, FINAL, PVEC = 16, 17, 18, 19, 20
+    S_PIECE, S_TWIN, S_RSUM, S_CSUM, S_DSUM, S_FINAL, S_SWAP = 0, 1, 2, 3, 4, 5, 6
+    S_PANEL, S_TRIAL, S_VECTOR, S_PART, S_COLUMN = 7, 8, 16, 24, 25
 
     def lane(expanded, s):
         return expanded[:, s * 128 : (s + 1) * 128]
@@ -150,6 +153,16 @@
             w_sem.at[number],
         )
 
+    def stage_copies():
+        copies = []
+        for half in range(2):
+            for t in range(LINES):
+                source = bands.at[t, pl.ds(first + half * (WIDTH // 2), WIDTH // 2)]
+                number = half * LINES + t
+                place = stage.at[half, pl.ds(t * (WIDTH // 2), WIDTH // 2)]
+                copies.append(pltpu.make_async_copy(source, place, local.at[1 + number]))
+        return copies
+
     def fetch_density():
         return pltpu.make_async_copy(density, dens, local.at[0])
 
@@ -160,7 +173,8 @@
 
     def unpack_piece(half, source):
         for t in range(LINES):
-            value = pieces[half, source, t].astype(F32).reshape(WIDTH * 4, 256)
+            lines = slice(t * (WIDTH // 2), (t + 1) * (WIDTH // 2))
+            value = pieces[half, source, lines].astype(F32).reshape(WIDTH * 4, 256)
             base = pl.multiple_of((t * SIDE + source * WIDTH + half * (WIDTH // 2)) * 8, 8)
             for h in range(2):
                 flat[h, pl.ds(base, WIDTH * 4), :] = value[:, halves[h]]
@@ -188,9 +202,9 @@
             line = HALF * LINES + col * LINES + e + rows
             for source in range(ROWS):
                 for half in range(2):
+                    wide = pieces[half, source, BLOCKS - 1].astype(F32)
                     for i in range(WIDTH // 2):
-                        held = pieces[half, source, LINES, i].astype(F32)
-                        held = jnp.where((places == line) & (rows < LINES), held, 0.0)
+                        held = jnp.where((places == line + 64 * i) & (rows < LINES), wide, 0.0)
                         factor = jnp.sum(held, axis=1, keepdims=True)
                         factor = jnp.broadcast_to(factor, (8, 128))
                         b = source * WIDTH + half * (WIDTH // 2) + i
@@ -233,53 +247,51 @@
                     y_col[h, (a * 4 + c) * 8 : (a * 4 + c) * 8 + 8, :] = total
         c_sum[...] = jnp.zeros_like(c_sum)
 
-    def one_block(q_value, carry):
+    def one_block(q_value):
         start = lax.rem(first + SIDE - q_value, SIDE)
         inside = (first + iota((8, 128), 0) >= q_value) | (col > 0)
         same = (q_value == 0) & (col == 0)
-        for t in range(LINES):
-
-            def rows(table, c, h):
-                return table[h, pl.ds((t * 4 + c) * RING + start, 8), :]
-
-            lefts = [[rows(left_t, c, h) for h in range(2)] for c in range(4)]
-            backs = [[rows(y_row, c, h) for h in range(2)] for c in range(4)]
-            totals = [[None, None] for _ in range(4)]
-            for e in range(LINES):
+
+        def rows(table, t, c, h):
+            return table[h, pl.ds((t * 4 + c) * RING + start, 8), :]
+
+        for e in range(LINES):
+            tiles = []
+            for t in range(LINES):
                 a = t + e
                 factor = keep_t[pl.ds((e * LINES + t) * RING + start, 8), :]
                 if e == 0:
                     factor = jnp.where(inside, factor, 0.0)
-                tiles = []
                 for c in range(4):
                     both = []
                     for h in range(2):
-                        kept = lefts[c][h] * factor
+                        kept = rows(left_t, t, c, h) * factor
                         both.append(jnp.concatenate([kept, kept], axis=0).astype(BF16))
                     both = jnp.concatenate(both, axis=1)
                     for pair in range(2):
                         base = a * 32 + pair * 16
                         tiles.append(both * u_col[base : base + 16, :])
-                mixed = dot(jnp.concatenate(tiles, axis=0), w_buf[e, q_value])
+            mixed = dot(jnp.concatenate(tiles, axis=0), w_buf[e, q_value])
+            for t in range(LINES):
+                a = t + e
                 for h in range(2):
                     images = [None] * 4
                     for c in range(4):
+                        total = None
+                        back = rows(y_row, t, c, h)
                         for d in range(4):
-                            base = (c * 4 + d) * 8
+                            base = t * 128 + (c * 4 + d) * 8
                             piece = mixed[base : base + 8, halves[h]]
                             base = (a * 4 + d) * 8
                             part = piece * y_col[h, base : base + 8, :]
-                            totals[c][h] = part if totals[c][h] is None else totals[c][h] + part
-                            part = piece * backs[c][h]
+                            total = part if total is None else total + part
+                            part = piece * back
                             images[d] = part if images[d] is None else images[d] + part
+                        r_sum[h, pl.ds((t * 4 + c) * RING + start, 8), :] += total
                     for d in range(4):
                         base = (a * 4 + d) * 8
                         image = jnp.where(same, 0.0, images[d]) if e == 0 else images[d]
                         c_sum[h, base : base + 8, :] += image
-            for c in range(4):
-                for h in range(2):
-                    r_sum[h, pl.ds((t * 4 + c) * RING + start, 8), :] += totals[c][h]
-        return carry
 
     def finish():
         lanes = iota((SIDE, 128), 1)
@@ -387,52 +399,49 @@
         copies = []
         for step in range(1, 2 * HALF):
             peer = lax.rem(col + step, 2 * HALF)
-            copies.append(to(ssum, fbuf.at[col], S_FINAL + step, FINAL + col, (row, peer)))
+            copies.append(to(ssum, fbuf.at[col], S_FINAL, FINAL, (row, peer)))
         return copies
 
-    def half_panel(half):
-        return bands.at[:, pl.ds(first + half * (WIDTH // 2), WIDTH // 2)]
-
     def panel_copies():
-        return [
-            to(half_panel(j % 2), pieces.at[j % 2, row, 0:LINES], j, OWN, (row, j))
-            for j in range(HALF)
-        ] + [to(trial, ptrial, 8 + j, PT, (row, j)) for j in range(HALF)]
+        return [to(stage.at[j % 2], pieces.at[j % 2, row], S_PANEL, OWN, (row, j)) for j in range(HALF)]
+
+    def trial_copies():
+        return [to(trial, ptrial, S_TRIAL + j, PT, (row, j)) for j in range(HALF)]
 
     def column_copies():
         near = (row, lax.rem(col + HALF, 2 * HALF))
         own = bands.at[:, pl.ds(first, WIDTH)]
         return [
-            to(own, cols.at[0:LINES], 16, COLS, near),
-            to(trial, ctrial.at[0], 17, CT, near),
+            to(own, cols.at[0:LINES], S_COLUMN, COLS, near),
+            to(trial, ctrial.at[0], S_COLUMN + 1, CT, near),
         ]
 
     def next_copies():
         far = (row, lax.rem(col + HALF - 1, 2 * HALF))
         own = bands.at[0 : LINES - 1, pl.ds(first, WIDTH)]
         return [
-            to(own, cols.at[LINES:SLOTS], 18, NEXT, far),
-            to(trial, ctrial.at[1], 19, CTN, far),
+            to(own, cols.at[LINES:SLOTS], S_COLUMN + 2, NEXT, far),
+            to(trial, ctrial.at[1], S_COLUMN + 3, CTN, far),
         ]
 
     def vector_copies():
-        return [to(rsend, rvec, 20 + j, RVEC, (row, HALF + j)) for j in range(1, HALF)]
+        return [to(rsend, rvec, S_VECTOR + j, RVEC, (row, HALF + j)) for j in range(1, HALF)]
 
     def piece_copies():
         own = pieces.at[core, row]
-        return [to(own, own, S_TWIN, TWIN, twin)] + [
-            to(own, own, S_PIECE + step, PIECE + step, (peer, col)) for step, peer in row_peers()
-        ]
+        return [
+            to(own, own, S_PIECE, PIECE + step, (peer, col)) for step, peer in row_peers()
+        ] + [to(own, own, S_TWIN, TWIN, twin)]
 
     def twin_copies():
         return [
-            to(pieces.at[core, source], pieces.at[core, source], S_TWIN + step, TWIN + step, twin)
+            to(pieces.at[core, source], pieces.at[core, source], S_TWIN, TWIN, twin)
             for step, source in row_sources()
         ]
 
     def sum_copies():
         return [
-            to(zrow.at[peer], rbuf.at[row], S_RSUM + step, RSUM + step, (peer, col))
+            to(zrow.at[peer], rbuf.at[step - 1], S_RSUM, RSUM, (peer, col))
             for step, peer in row_peers()
         ]
 
@@ -446,22 +455,32 @@
 
     def exchange_copies():
         return [
-            to(zex.at[peer], ebuf.at[row], S_SWAP + step, RSUM + step, (peer, col))
+            to(zex.at[peer], ebuf.at[step - 1], S_SWAP, RSUM, (peer, col))
             for step, peer in row_peers()
         ]
 
     def part_copy():
-        return to(pvec, pbuf.at[col - HALF], 8, PVEC + col - HALF, (row, HALF))
+        return to(pvec, pbuf.at[col - HALF], S_PART, PVEC + col - HALF, (row, HALF))
 
     @pl.when(col < HALF)
     def _():
         for number in range(SIDE // Q_STEP):
             chunk(number).start()
-        for i in range(WIDTH // 2):
-            held = jnp.where(core == 0, window[:, i], window[:, WIDTH // 2 + i]).astype(F32)
-            held = jnp.concatenate([held, jnp.zeros((8 - LINES, SIDE), F32)], axis=0)
-            held = jnp.concatenate([held, jnp.zeros((8, 256 - SIDE), F32)], axis=1)
-            pieces[core, row, LINES, i] = held.astype(BF16)
+
+    @pl.when(col == HALF)
+    def _():
+        for copy in stage_copies():
+            copy.start()
+        for half in range(2):
+            parts = []
+            for i in range(WIDTH // 2):
+                held = window[:, half * (WIDTH // 2) + i].astype(F32)
+                held = jnp.concatenate([held, jnp.zeros((8 - LINES, SIDE), F32)], axis=0)
+                parts.append(jnp.concatenate([held, jnp.zeros((8, 64 - SIDE), F32)], axis=1))
+            parts.append(jnp.zeros((8, 64), F32))
+            stage[half, BLOCKS - 1] = jnp.concatenate(parts, axis=1).astype(BF16)
+        for copy in stage_copies():
+            copy.wait()
 
     @pl.when(col >= HALF)
     def _():
@@ -471,38 +490,41 @@
 
     @pl.when(col < HALF)
     def _():
-        to(half_panel(0), pieces.at[core, row, 0:LINES], 0, OWN, (row, HALF)).wait_recv()
+        own = pieces.at[core, row]
+        to(own, own, 0, OWN, (row, HALF)).wait_recv()
         for copy in piece_copies():
             copy.start()
-        to(cols.at[0:LINES], cols.at[0:LINES], 0, COLS, (row, HALF)).wait_recv()
-        to(trial, ctrial.at[0], 0, CT, (row, HALF)).wait_recv()
-
-        @pl.when(col < HALF - 1)
-        def _():
-            to(cols.at[LINES:SLOTS], cols.at[LINES:SLOTS], 0, NEXT, (row, HALF)).wait_recv()
-            to(trial, ctrial.at[1], 0, CTN, (row, HALF)).wait_recv()
-
-        prepare_columns()
-        unpack_piece(core, row)
-        forwards = twin_copies()
-        for (step, source), forward in zip(row_sources(), forwards):
+        for (step, source), forward in zip(row_sources(), twin_copies()):
             piece = pieces.at[core, source]
             to(piece, piece, 0, PIECE + step, (source, col)).wait_recv()
             forward.start()
+        to(cols.at[0:LINES], cols.at[0:LINES], 0, COLS, (row, HALF)).wait_recv()
+        to(trial, ctrial.at[0], 0, CT, (row, HALF)).wait_recv()
+
+        @pl.when(col < HALF - 1)
+        def _():
+            to(cols.at[LINES:SLOTS], cols.at[LINES:SLOTS], 0, NEXT, (row, HALF)).wait_recv()
+            to(trial, ctrial.at[1], 0, CTN, (row, HALF)).wait_recv()
+
+        prepare_columns()
+        for source in range(ROWS):
             unpack_piece(core, source)
-        piece = pieces.at[1 - core, row]
-        to(piece, piece, 0, TWIN, twin).wait_recv()
-        unpack_piece(1 - core, row)
-        for step, source in row_sources():
-            piece = pieces.at[1 - core, source]
-            to(piece, piece, 0, TWIN + step, twin).wait_recv()
+        other = pieces.at[1 - core]
+        to(other, other, 0, TWIN, twin).wait_recv()
+        for source in range(ROWS):
             unpack_piece(1 - core, source)
         to(trial, ptrial, 0, PT, (row, HALF)).wait_recv()
         prepare_panel()
+        sent = pieces.at[core, 0 : ROWS - 1]
+        to(sent, sent, S_PIECE, 0, twin).wait_send()
+        sent = pieces.at[core]
+        to(sent, sent, S_TWIN, 0, twin).wait_send()
 
         def one_chunk(number, carry):
             chunk(number).wait()
-            return lax.fori_loop(number * Q_STEP, (number + 1) * Q_STEP, one_block, carry)
+            for k in range(Q_STEP):
+                one_block(number * Q_STEP + k)
+            return carry
 
         lax.fori_loop(0, SIDE // Q_STEP, one_chunk, 0)
         finish()
@@ -514,25 +536,17 @@
         def _():
             far_sum().start()
 
+        to(rbuf, rbuf, 0, RSUM, twin).wait_recv()
         total = zrow[row]
-        for step, source in row_sources():
-            to(zrow.at[0], rbuf.at[source], 0, RSUM + step, (source, col)).wait_recv()
-            total += rbuf[source]
+        for step in range(ROWS - 1):
+            total += rbuf[step]
         ssum[...] = total
 
     @pl.when(col >= HALF)
     def _():
         @pl.when(col == HALF)
         def _():
-            for copy in panel_copies():
-                copy.start()
-
-        for copy in column_copies():
-            copy.start()
-
-        @pl.when(col > HALF)
-        def _():
-            for copy in next_copies():
+            for copy in panel_copies() + trial_copies():
                 copy.start()
 
         fetch_density().wait()
@@ -547,6 +561,11 @@
         @pl.when(col > HALF)
         def _():
             to(rsend, rvec, 0, RVEC, (row, HALF)).wait_recv()
+            for copy in next_copies():
+                copy.start()
+
+        for copy in column_copies():
+            copy.start()
 
         exchange()
         for copy in exchange_copies():
@@ -570,91 +589,102 @@
 
     @pl.when(col < HALF)
     def _():
-        col_image[...] = jnp.zeros_like(col_image)
+        col_part[...] = jnp.zeros_like(col_part)
 
     @pl.when(col >= HALF)
     def _():
+        to(ebuf, ebuf, 0, RSUM, (row, HALF)).wait_recv()
         swapped = zex[row]
-        for step, source in row_sources():
-            to(zex.at[0], ebuf.at[source], 0, RSUM + step, (source, col)).wait_recv()
-            swapped += ebuf[source]
+        for step in range(ROWS - 1):
+            swapped += ebuf[step]
+        for copy in column_copies():
+            copy.wait_send()
+        to(ebuf, ebuf, S_SWAP, 0, twin).wait_send()
+
+        @pl.when(col > HALF)
+        def _():
+            for copy in next_copies() + [part_copy()]:
+                copy.wait_send()
+
+        @pl.when(col == HALF)
+        def _():
+            to(pieces.at[0], pieces.at[0], S_PANEL, 0, twin).wait_send()
+            for copy in trial_copies() + vector_copies():
+                copy.wait_send()
+
+        fold = ones_where(iota((128, 128), 0) % 16 == iota((128, 128), 1), F32)
+        spots = iota((8, 128), 1) // 16 == iota((8, 128), 0)
+        images = []
+        for a in range(LINES):
+            images.append(dot(jnp.where(spots, swapped[a : a + 1], 0.0), fold, precision=HIGHEST))
         to(zcol.at[0:LINES], cbuf, 0, CSUM, (row, HALF)).wait_recv()
 
         @pl.when(col > HALF)
         def _():
             to(zcol.at[LINES:SLOTS], dbuf, 0, DSUM, (row, HALF)).wait_recv()
 
-        picks = ones_where(iota((16, 128), 0) == iota((16, 128), 1), F32)
-        folds = iota((16, 128), 1) % 16 == iota((16, 128), 0)
-        spots = ones_where(iota((8, 128), 1) // 16 == iota((8, 128), 0), F32)
         for a in range(LINES):
-            direct = cbuf[a]
+            image = images[a] + cbuf[a]
             if a < LINES - 1:
-                direct += jnp.where(col > HALF, dbuf[a], 0.0)
-            image = dot(picks, direct, (1, 1), HIGHEST)
-            values = jnp.where(folds, swapped[a : a + 1], 0.0)
-            image += dot(values, spots, (1, 1), HIGHEST)
-            col_image[:, a, :] = image[:, 0:WIDTH]
-
-    for source in range(HALF + 1):
-
-        @pl.when(col != source)
-        def _():
-            to(ssum, fbuf.at[source], 0, FINAL + source, (row, source)).wait_recv()
+                image += jnp.where(col > HALF, dbuf[a], 0.0)
+            col_part[a] = image
+
+    @pl.when(col <= HALF)
+    def _():
+        to(fbuf.at[0:HALF], fbuf.at[0:HALF], 0, FINAL, twin).wait_recv()
+
+    @pl.when(col > HALF)
+    def _():
+        to(fbuf.at[0 : HALF + 1], fbuf.at[0 : HALF + 1], 0, FINAL, twin).wait_recv()
 
     total = fbuf[0]
     for source in range(1, HALF + 1):
         total += fbuf[source]
-    choose = ones_where(iota((8, 128), 1) == iota((8, 128), 0) * 16 + col, F32)
-    picked = dot(choose, total, (1, 1), HIGHEST)
-    row_image[0] = picked[0:LINES, 0:WIDTH]
+    row_part[...] = total
 
     @pl.when(col < HALF)
     def _():
-        for copy in piece_copies() + twin_copies() + sum_copies() + [near_sum()]:
-            copy.wait_send()
+        to(rbuf, rbuf, S_RSUM, 0, twin).wait_send()
+        near_sum().wait_send()
 
         @pl.when(col < HALF - 1)
         def _():
             far_sum().wait_send()
 
-    @pl.when(col >= HALF)
-    def _():
-        for copy in column_copies() + exchange_copies():
-            copy.wait_send()
-
-        @pl.when(col > HALF)
-        def _():
-            for copy in next_copies() + [part_copy()]:
-                copy.wait_send()
-
-        @pl.when(col == HALF)
-        def _():
-            for copy in panel_copies() + vector_copies():
-                copy.wait_send()
-
     @pl.when(col <= HALF)
     def _():
-        for copy in final_copies():
-            copy.wait_send()
+        sent = fbuf.at[0 : 2 * HALF - 1]
+        to(sent, sent, S_FINAL, 0, twin).wait_send()
+
+
+def place_kernel(row_part, col_part, row_image, col_image):
+    choose = ones_where(
+        iota((8, 128), 1) == iota((8, 128), 0) * 16 + lax.axis_index("col"), F32
+    )
+    picked = dot(choose, row_part[...], (1, 1), HIGHEST)
+    for t in range(LINES):
+        row_image[t] = picked[t : t + 1, 0:WIDTH]
+    for a in range(LINES):
+        col_image[a] = col_part[a, 0:WIDTH, 0:16]
 
 
 def local(band_factors, pair_density, screened, coulomb, window_mask, trial_vector):
     trial = trial_vector.transpose(1, 0, 2)
     vmem = pltpu.VMEM
-    row_image, col_image = pl.pallas_call(
+    parts = pl.pallas_call(
         panel_product_kernel,
         name="panel_product",
         out_shape=[
-            jax.ShapeDtypeStruct((1, LINES, WIDTH), F32),
-            jax.ShapeDtypeStruct((16, LINES, WIDTH), F32),
+            jax.ShapeDtypeStruct((8, 128), F32),
+            jax.ShapeDtypeStruct((LINES, 8, 128), F32),
         ],
         in_specs=[ANY, ANY, ANY, ANY, VMEM, VMEM, VMEM],
         out_specs=[VMEM, VMEM],
         scratch_shapes=[
             vmem((LINES, SIDE, 256, 256), BF16),
             vmem((LINES, SIDE, 16, 256), BF16),
-            vmem((2, ROWS, LINES + 1, WIDTH // 2, 8, 256), BF16),
+            vmem((2, BLOCKS, 8, 256), BF16),
+            vmem((2, ROWS, BLOCKS, 8, 256), BF16),
             vmem((SLOTS, WIDTH, 8, 256), BF16),
             vmem((2, LINES, 16, SIDE), BF16),
             vmem((LINES, 16, SIDE), BF16),
@@ -673,16 +703,16 @@
             vmem((SLOTS, 8, 128), F32),
             vmem((LINES, 8, 256), F32),
             vmem((ROWS, 8, 128), F32),
-            vmem((ROWS, 8, 128), F32),
+            vmem((ROWS - 1, 8, 128), F32),
             vmem((LINES, 8, 128), F32),
             vmem((SLOTS - LINES, 8, 128), F32),
             vmem((HALF, LINES, 8, 256), F32),
-            vmem((ROWS, 8, 128), F32),
-            vmem((HALF + 1, 8, 128), F32),
+            vmem((ROWS - 1, 8, 128), F32),
+            vmem((2 * HALF, 8, 128), F32),
             vmem((8, 128), F32),
-            pltpu.SemaphoreType.DMA((56,)),
-            pltpu.SemaphoreType.DMA((52,)),
-            pltpu.SemaphoreType.DMA((1,)),
+            pltpu.SemaphoreType.DMA((29,)),
+            pltpu.SemaphoreType.DMA((28,)),
+            pltpu.SemaphoreType.DMA((7,)),
             pltpu.SemaphoreType.DMA((SIDE // Q_STEP,)),
         ],
         compiler_params=pltpu.CompilerParams(
@@ -697,7 +727,17 @@
         trial,
         coulomb.reshape(1, 256),
     )
-    return row_image, col_image
+    row_image, col_image = pl.pallas_call(
+        place_kernel,
+        name="place",
+        out_shape=[
+            jax.ShapeDtypeStruct((LINES, 1, WIDTH), F32),
+            jax.ShapeDtypeStruct((LINES, WIDTH, 16), F32),
+        ],
+        in_specs=[VMEM, VMEM],
+        out_specs=[VMEM, VMEM],
+    )(*parts)
+    return row_image.transpose(1, 0, 2), col_image.transpose(2, 0, 1)
 
 
 def solution(mesh):

time: 56 us -> 50.3 us (0.90)
  Pallas kernels: 52.4 us -> 49.3 us
  local copies, waits for them, and re-layouts: 2.67 us -> 0 us
    pallas_call x1, Pallas kernels: 52.4 us -> 47.8 us  [local(): pl.pallas_call(panel_product_kernel, name='panel_product', out_shape=[jax...]
    pallas_call x2 -> x0, local copies, waits for them, and re-layouts: 2.67 us -> none  [local(): pl.pallas_call(panel_product_kernel, name='panel_product', out_shape=[jax...]
    pallas_call x0 -> x1, Pallas kernels: none -> 1.42 us  [local(): pl.pallas_call(place_kernel, name='place', out_shape=[jax.ShapeDtypeStruc...]
where the time goes in v3:
time: 50.3 us; the launch traced here: 49.9 us
  Pallas kernels  49.3 us (98%)
  between operations  0.64 us (1%)
    pallas_call x1, Pallas kernels, local(): pl.pallas_call(panel_product_kernel, name='panel_product', out_shape=[jax...  47.8 us
    pallas_call x1, Pallas kernels, local(): pl.pallas_call(place_kernel, name='place', out_shape=[jax.ShapeDtypeStruc...  1.42 us

profile of v3, /device:TPU:1, one launch (start us, length us, event | category | flops | bytes accessed | tf_op | source)
XLA Modules:
  0.0 49.9 jit_solution(3293106578971830533)
XLA Ops:
  0.6 47.8 %panel_product.1 = (f32[8,128]{1,0:T(8,128)}, f32[3,8,128]{2,1,0:T(8,128)}) custom-call(bf16[3,48,8,256]{3,2,1,0:T(8,128)(2,1)} %bands.1, bf16[3,48,16,256]{3,2,1,0:T(8,128)(2,1)} %density.1, bf16[3,48,256,256]{3,2,1,0:T(8,128)(2,1)} %blocks.1, bf16[3,16,48]{2,1,0:T(8,128)(2,1)} %bitcast.4, s32[3,6,48]{2,1,0:T(8,128)} %window.1, bf16[3,16,48]{2,1,0:T(8,128)(2,1)} %bitcast.5, ...), custom_call_target="tpu_custom_call" | custom-call | tf_op jit(solution)/shard_map/panel_product/pallas_call | solution.py:674
  48.5 1.4 %place.1 = (f32[3,1,6]{2,1,0:T(1,128)}, f32[3,6,16]{2,1,0:T(8,128)}) custom-call(f32[8,128]{1,0:T(8,128)} %get-tuple-element.6.row_part, f32[3,8,128]{2,1,0:T(8,128)} %get-tuple-element.7.col_part), custom_call_target="tpu_custom_call" | custom-call | tf_op jit(solution)/shard_map/place/pallas_call | solution.py:730

commit v4 on v3

--- a/solution.py
+++ b/solution.py
@@ -133,10 +133,10 @@
         return remote(source, target, send.at[number], recv.at[arrives], device)
 
     def row_peers():
-        return [(step, lax.rem(row + step, ROWS)) for step in range(1, ROWS)]
+        return [(step, lax.rem(row + step, ROWS)) for step in (5, 3, 7, 1, 4, 2, 6)]
 
     def row_sources():
-        return [(step, lax.rem(row + ROWS - step, ROWS)) for step in range(1, ROWS)]
+        return [(step, lax.rem(row + ROWS - step, ROWS)) for step in (2, 6, 4, 1, 7, 3, 5)]
 
     COLS, NEXT, CT, CTN, PT, OWN, RVEC, TWIN, PIECE = 0, 1, 2, 3, 4, 5, 6, 7, 8
     RSUM, CSUM, DSUM, FINAL, PVEC = 16, 17, 18, 19, 20
@@ -397,7 +397,7 @@
 
     def final_copies():
         copies = []
-        for step in range(1, 2 * HALF):
+        for step in (8, 9, 10, 11, 7, 6, 5, 4, 12, 13, 14, 15, 3, 2, 1):
             peer = lax.rem(col + step, 2 * HALF)
             copies.append(to(ssum, fbuf.at[col], S_FINAL, FINAL, (row, peer)))
         return copies
@@ -546,13 +546,23 @@
     def _():
         @pl.when(col == HALF)
         def _():
-            for copy in panel_copies() + trial_copies():
+            for copy in panel_copies():
                 copy.start()
 
+        for copy in column_copies():
+            copy.start()
+
+        @pl.when(col > HALF)
+        def _():
+            for copy in next_copies():
+                copy.start()
+
         fetch_density().wait()
 
         @pl.when(col == HALF)
         def _():
+            for copy in trial_copies():
+                copy.start()
             row_vectors()
             for copy in vector_copies():
                 copy.start()
@@ -561,11 +571,6 @@
         @pl.when(col > HALF)
         def _():
             to(rsend, rvec, 0, RVEC, (row, HALF)).wait_recv()
-            for copy in next_copies():
-                copy.start()
-
-        for copy in column_copies():
-            copy.start()
 
         exchange()
         for copy in exchange_copies():

time: 50.3 us -> 49.4 us (0.982)
  Pallas kernels: 49.3 us -> 48.4 us
    pallas_call x1, Pallas kernels: 47.8 us -> 47 us  [local(): pl.pallas_call(panel_product_kernel, name='panel_product', out_shape=[jax...]
where the time goes in v4:
time: 49.4 us; the launch traced here: 49 us
  Pallas kernels  48.4 us (98%)
  between operations  0.64 us (1%)
    pallas_call x1, Pallas kernels, local(): pl.pallas_call(panel_product_kernel, name='panel_product', out_shape=[jax...  47 us
    pallas_call x1, Pallas kernels, local(): pl.pallas_call(place_kernel, name='place', out_shape=[jax.ShapeDtypeStruc...  1.42 us

profile of v4, /device:TPU:1, one launch (start us, length us, event | category | flops | bytes accessed | tf_op | source)
XLA Modules:
  0.0 49.0 jit_solution(2572075680106429324)
XLA Ops:
  0.6 47.0 %panel_product.1 = (f32[8,128]{1,0:T(8,128)}, f32[3,8,128]{2,1,0:T(8,128)}) custom-call(bf16[3,48,8,256]{3,2,1,0:T(8,128)(2,1)} %bands.1, bf16[3,48,16,256]{3,2,1,0:T(8,128)(2,1)} %density.1, bf16[3,48,256,256]{3,2,1,0:T(8,128)(2,1)} %blocks.1, bf16[3,16,48]{2,1,0:T(8,128)(2,1)} %bitcast.4, s32[3,6,48]{2,1,0:T(8,128)} %window.1, bf16[3,16,48]{2,1,0:T(8,128)(2,1)} %bitcast.5, ...), custom_call_target="tpu_custom_call" | custom-call | tf_op jit(solution)/shard_map/panel_product/pallas_call | solution.py:679
  47.6 1.4 %place.1 = (f32[3,1,6]{2,1,0:T(1,128)}, f32[3,6,16]{2,1,0:T(8,128)}) custom-call(f32[8,128]{1,0:T(8,128)} %get-tuple-element.6.row_part, f32[3,8,128]{2,1,0:T(8,128)} %get-tuple-element.7.col_part), custom_call_target="tpu_custom_call" | custom-call | tf_op jit(solution)/shard_map/place/pallas_call | solution.py:735

commit v5 on v4

--- a/solution.py
+++ b/solution.py
@@ -64,7 +64,6 @@
         pl.semaphore_signal(
             barrier, inc=1, device_id=(row, lax.rem(col + step, 2 * HALF)), device_id_type=MESH
         )
-    pl.semaphore_wait(barrier, ROWS + 2 * HALF - 2)
 
 
 def remote(source, target, send_sem, recv_sem, device):
@@ -104,7 +103,7 @@
     r_sum,
     col_flat,
     u_col,
-    y_col,
+    y_pair,
     c_sum,
     zrow,
     zcol,
@@ -240,11 +239,17 @@
                         BF16
                     )
                 valence = [band(4 + v) for v in range(4)]
+                totals = []
                 for c in range(4):
                     total = valence[0] * lane(expanded, c)
                     for v in range(1, 4):
                         total += valence[v] * lane(expanded, 4 * v + c)
-                    y_col[h, (a * 4 + c) * 8 : (a * 4 + c) * 8 + 8, :] = total
+                    totals.append(total)
+                for pair in range(2):
+                    both = jnp.concatenate([totals[2 * pair], totals[2 * pair + 1]], axis=0)
+                    y_pair[a * 32 + pair * 16 : a * 32 + pair * 16 + 16, halves[h]] = both.astype(
+                        BF16
+                    )
         c_sum[...] = jnp.zeros_like(c_sum)
 
     def one_block(q_value):
@@ -255,6 +260,12 @@
         def rows(table, t, c, h):
             return table[h, pl.ds((t * 4 + c) * RING + start, 8), :]
 
+        backs = []
+        for t in range(LINES):
+            backs.append([])
+            for c in range(4):
+                values = [rows(y_row, t, c, h) for h in range(2)]
+                backs[t].append([jnp.concatenate([x, x], axis=0).astype(BF16) for x in values])
         for e in range(LINES):
             tiles = []
             for t in range(LINES):
@@ -271,29 +282,30 @@
                     for pair in range(2):
                         base = a * 32 + pair * 16
                         tiles.append(both * u_col[base : base + 16, :])
-            mixed = dot(jnp.concatenate(tiles, axis=0), w_buf[e, q_value])
+            mixed = dot(jnp.concatenate(tiles, axis=0), w_buf[e, q_value]).astype(BF16)
             for t in range(LINES):
                 a = t + e
                 for h in range(2):
-                    images = [None] * 4
+                    products = [[], []]
                     for c in range(4):
-                        total = None
-                        back = rows(y_row, t, c, h)
-                        for d in range(4):
-                            base = t * 128 + (c * 4 + d) * 8
-                            piece = mixed[base : base + 8, halves[h]]
-                            base = (a * 4 + d) * 8
-                            part = piece * y_col[h, base : base + 8, :]
-                            total = part if total is None else total + part
-                            part = piece * back
-                            images[d] = part if images[d] is None else images[d] + part
-                        r_sum[h, pl.ds((t * 4 + c) * RING + start, 8), :] += total
-                    for d in range(4):
-                        base = (a * 4 + d) * 8
-                        image = jnp.where(same, 0.0, images[d]) if e == 0 else images[d]
-                        c_sum[h, base : base + 8, :] += image
-
-    def finish():
+                        parts = []
+                        for pair in range(2):
+                            base = t * 128 + c * 32 + pair * 16
+                            piece = mixed[base : base + 16, halves[h]]
+                            base = a * 32 + pair * 16
+                            parts.append(piece * y_pair[base : base + 16, halves[h]])
+                            products[pair].append(piece * backs[t][c][h])
+                        total = (parts[0] + parts[1]).astype(F32)
+                        r_sum[h, pl.ds((t * 4 + c) * RING + start, 8), :] += total[0:8] + total[8:16]
+                    for pair in range(2):
+                        some = products[pair]
+                        image = ((some[0] + some[1]) + (some[2] + some[3])).astype(F32)
+                        if e == 0:
+                            image = jnp.where(same, 0.0, image)
+                        base = a * 32 + pair * 16
+                        c_sum[h, base : base + 16, :] += image
+
+    def finish_rows():
         lanes = iota((SIDE, 128), 1)
         image = jnp.zeros((SIDE, 128), F32)
         for t in range(LINES):
@@ -315,6 +327,8 @@
         for target in range(ROWS):
             zrow[target, 0:WIDTH, :] = -image[target * WIDTH : (target + 1) * WIDTH]
             zrow[target, WIDTH:8, :] = jnp.zeros((8 - WIDTH, 128), F32)
+
+    def finish_columns():
         lanes = iota((8, 128), 1)
         for a in range(SLOTS):
             image = jnp.zeros((8, 128), F32)
@@ -462,6 +476,8 @@
     def part_copy():
         return to(pvec, pbuf.at[col - HALF], S_PART, PVEC + col - HALF, (row, HALF))
 
+    greet()
+
     @pl.when(col < HALF)
     def _():
         for number in range(SIDE // Q_STEP):
@@ -486,7 +502,7 @@
     def _():
         fetch_density().start()
 
-    greet()
+    pl.semaphore_wait(pltpu.get_barrier_semaphore(), ROWS + 2 * HALF - 2)
 
     @pl.when(col < HALF)
     def _():
@@ -527,9 +543,10 @@
             return carry
 
         lax.fori_loop(0, SIDE // Q_STEP, one_chunk, 0)
-        finish()
+        finish_rows()
         for copy in sum_copies():
             copy.start()
+        finish_columns()
         near_sum().start()
 
         @pl.when(col < HALF - 1)
@@ -702,7 +719,7 @@
             vmem((2, LINES * 4 * RING, 128), F32),
             vmem((2, SLOTS * 64, 128), F32),
             vmem((SLOTS * 32, 256), BF16),
-            vmem((2, SLOTS * 32, 128), F32),
+            vmem((SLOTS * 32, 256), BF16),
             vmem((2, SLOTS * 32, 128), F32),
             vmem((ROWS, 8, 128), F32),
             vmem((SLOTS, 8, 128), F32),

time: 49.4 us -> 48.6 us (0.984)
  Pallas kernels: 48.4 us -> 47.6 us
    pallas_call x1, Pallas kernels: 47 us -> 46.2 us  [local(): pl.pallas_call(panel_product_kernel, name='panel_product', out_shape=[jax...]
where the time goes in v5:
time: 48.6 us; the launch traced here: 48.2 us
  Pallas kernels  47.6 us (98%)
  between operations  0.64 us (1%)
    pallas_call x1, Pallas kernels, local(): pl.pallas_call(panel_product_kernel, name='panel_product', out_shape=[jax...  46.2 us
    pallas_call x1, Pallas kernels, local(): pl.pallas_call(place_kernel, name='place', out_shape=[jax.ShapeDtypeStruc...  1.42 us

profile of v5, /device:TPU:1, one launch (start us, length us, event | category | flops | bytes accessed | tf_op | source)
XLA Modules:
  0.0 48.2 jit_solution(3359167722388017677)
XLA Ops:
  0.6 46.2 %panel_product.1 = (f32[8,128]{1,0:T(8,128)}, f32[3,8,128]{2,1,0:T(8,128)}) custom-call(bf16[3,48,8,256]{3,2,1,0:T(8,128)(2,1)} %bands.1, bf16[3,48,16,256]{3,2,1,0:T(8,128)(2,1)} %density.1, bf16[3,48,256,256]{3,2,1,0:T(8,128)(2,1)} %blocks.1, bf16[3,16,48]{2,1,0:T(8,128)(2,1)} %bitcast.4, s32[3,6,48]{2,1,0:T(8,128)} %window.1, bf16[3,16,48]{2,1,0:T(8,128)(2,1)} %bitcast.5, ...), custom_call_target="tpu_custom_call" | custom-call | tf_op jit(solution)/shard_map/panel_product/pallas_call | solution.py:696
  46.8 1.4 %place.1 = (f32[3,1,6]{2,1,0:T(1,128)}, f32[3,6,16]{2,1,0:T(8,128)}) custom-call(f32[8,128]{1,0:T(8,128)} %get-tuple-element.6.row_part, f32[3,8,128]{2,1,0:T(8,128)} %get-tuple-element.7.col_part), custom_call_target="tpu_custom_call" | custom-call | tf_op jit(solution)/shard_map/place/pallas_call | solution.py:752

commit v6 on v5

--- a/solution.py
+++ b/solution.py
@@ -18,7 +18,7 @@
 SLOTS = 2 * LINES - 1
 RING = SIDE + 8
 BLOCKS = LINES * WIDTH // 2 + 1
-Q_STEP = 4
+Q_STEP = 6
 HIGHEST = lax.Precision.HIGHEST
 ANY = pl.BlockSpec(memory_space=pl.ANY)
 VMEM = pl.BlockSpec(memory_space=pltpu.VMEM)
@@ -56,11 +56,11 @@
 def greet():
     row, col = lax.axis_index("row"), lax.axis_index("col")
     barrier = pltpu.get_barrier_semaphore()
-    for step in range(1, ROWS):
+    for step in (5, 3, 7, 1, 4, 2, 6):
         pl.semaphore_signal(
             barrier, inc=1, device_id=(lax.rem(row + step, ROWS), col), device_id_type=MESH
         )
-    for step in range(1, 2 * HALF):
+    for step in (8, 9, 10, 11, 7, 6, 5, 4, 12, 13, 14, 15, 3, 2, 1):
         pl.semaphore_signal(
             barrier, inc=1, device_id=(row, lax.rem(col + step, 2 * HALF)), device_id_type=MESH
         )

time: 48.6 us -> 48.4 us (level)
  no operation moved by 1% of the time
where the time goes in v6:
time: 48.4 us; the launch traced here: 48.1 us
  Pallas kernels  47.4 us (98%)
  between operations  0.64 us (1%)
    pallas_call x1, Pallas kernels, local(): pl.pallas_call(panel_product_kernel, name='panel_product', out_shape=[jax...  46 us
    pallas_call x1, Pallas kernels, local(): pl.pallas_call(place_kernel, name='place', out_shape=[jax.ShapeDtypeStruc...  1.42 us

profile of v6, /device:TPU:1, one launch (start us, length us, event | category | flops | bytes accessed | tf_op | source)
XLA Modules:
  0.0 48.1 jit_solution(3397814540589250772)
XLA Ops:
  0.6 46.0 %panel_product.1 = (f32[8,128]{1,0:T(8,128)}, f32[3,8,128]{2,1,0:T(8,128)}) custom-call(bf16[3,48,8,256]{3,2,1,0:T(8,128)(2,1)} %bands.1, bf16[3,48,16,256]{3,2,1,0:T(8,128)(2,1)} %density.1, bf16[3,48,256,256]{3,2,1,0:T(8,128)(2,1)} %blocks.1, bf16[3,16,48]{2,1,0:T(8,128)(2,1)} %bitcast.4, s32[3,6,48]{2,1,0:T(8,128)} %window.1, bf16[3,16,48]{2,1,0:T(8,128)(2,1)} %bitcast.5, ...), custom_call_target="tpu_custom_call" | custom-call | tf_op jit(solution)/shard_map/panel_product/pallas_call | solution.py:696
  46.7 1.4 %place.1 = (f32[3,1,6]{2,1,0:T(1,128)}, f32[3,6,16]{2,1,0:T(8,128)}) custom-call(f32[8,128]{1,0:T(8,128)} %get-tuple-element.6.row_part, f32[3,8,128]{2,1,0:T(8,128)} %get-tuple-element.7.col_part), custom_call_target="tpu_custom_call" | custom-call | tf_op jit(solution)/shard_map/place/pallas_call | solution.py:752
